TPU v7x, 32 devices: a whole 2x2x4 slice. The times are simulated.
32 devices in a mesh: row: 4 (over z), col: 8 (over y, x, core).
Axes of the slice: x: 2, y: 2, z: 4, core: 2. Of those that a mesh axis runs over, the one named last changes fastest.
Arguments:
- object_amplitude: float32 [1024, 2048], P('row', 'col'), may hold values from 0.3 to 3
- object_phase: float32 [1024, 2048], P('row', 'col'), may hold values from -3.140625 to 3.140625
- probe: float32 [4, 2, 256, 256], replicated, may hold values from -6 to 6
- amplitudes: float32 [256, 256, 256], P(('row', 'col')), may hold values from 0.5 to 3
- positions: int32 [256, 2], P(('row', 'col')), may hold values from -64 to 64
Outputs:
- new_object: float32 [2, 1024, 2048], P(None, 'row', 'col')
- new_probe: float32 [4, 2, 256, 256], replicated
Inputs may be any that keep to these rules, and one draw needn't show every extreme that they name: `positions`: row and column offsets of each frame's first pixel from the first pixel of its owner tile f // 8, tiles row-major; both ends of the range occur.
All inputs are finite; a program needn't handle non-finite values.
Results may differ from a plain program's by a relative error of at most 0.0014.
The roundings to bfloat16 on the way count: a program that leaves them out, or rounds other values in their place, can miss the bound.
Values sent between devices are 32-bit elements; how exact they have to be, the bound alone decides.
A program may use at most 192 MiB of HBM per device.

v0:
```python
import math

import jax
import jax.numpy as jnp
from jax import lax
from jax.sharding import PartitionSpec as P

H = 64


def extended_2(block, sides, width):
    for axis, dim in sides:
        count = lax.axis_size(axis)
        forward = [(i, i + 1) for i in range(count - 1)]
        backward = [(target, source) for source, target in forward]
        low = lax.ppermute(
            lax.slice_in_dim(block, block.shape[dim] - width, None, axis=dim), axis, forward
        )
        high = lax.ppermute(lax.slice_in_dim(block, 0, width, axis=dim), axis, backward)
        block = jnp.concatenate([low, block, high], axis=dim)
    return block


def fourier_table(frame_side, exponent_sign):
    counter = jnp.arange(frame_side, dtype=jnp.int32)
    product = counter[:, None] * counter[None, :] % frame_side
    phase_angle = product.astype(jnp.float32) * (2.0 * math.pi / frame_side)
    norming = 1.0 / math.sqrt(frame_side)
    real_part = jnp.cos(phase_angle) * norming
    imaginary = exponent_sign * jnp.sin(phase_angle) * norming
    upper_rows = jnp.stack([real_part, -imaginary], axis=1)
    lower_rows = jnp.stack([imaginary, real_part], axis=1)
    return jnp.stack([upper_rows, lower_rows], axis=0).astype(jnp.bfloat16)


def transform(matrix, values):
    halfway = jnp.einsum("akcy,fmcyx->fmakx", matrix, values, preferred_element_type=jnp.float32)
    return jnp.einsum(
        "fmakx,blax->fmbkl",
        halfway.astype(jnp.bfloat16),
        matrix,
        preferred_element_type=jnp.float32,
    )


def frame_terms(patches, probe, measured, forward, inverse):
    object_real = patches[:, None, 0]
    object_imag = patches[:, None, 1]
    probe_real = probe[None, :, 0]
    probe_imag = probe[None, :, 1]
    exit_wave = jnp.stack(
        [
            probe_real * object_real - probe_imag * object_imag,
            probe_real * object_imag + probe_imag * object_real,
        ],
        axis=2,
    )
    spectrum = transform(forward, exit_wave.astype(jnp.bfloat16))
    intensity = jnp.sum(spectrum * spectrum, axis=(1, 2))
    factor = measured / jnp.maximum(jnp.sqrt(intensity), 1.0)
    corrected = (spectrum * factor[:, None, None]).astype(jnp.bfloat16)
    returned = transform(inverse, corrected)
    change = returned - exit_wave
    change_real = change[:, :, 0]
    change_imag = change[:, :, 1]
    object_gradient = jnp.stack(
        [
            jnp.sum(probe_real * change_real + probe_imag * change_imag, axis=1),
            jnp.sum(probe_real * change_imag - probe_imag * change_real, axis=1),
        ],
        axis=1,
    )
    probe_gradient = jnp.stack(
        [
            jnp.sum(object_real * change_real + object_imag * change_imag, axis=0),
            jnp.sum(object_real * change_imag - object_imag * change_real, axis=0),
        ],
        axis=1,
    )
    weight = jnp.sum(patches * patches, axis=(0, 1))
    return (object_gradient, probe_gradient, weight)


def shards(object_amplitude, object_phase, probe, amplitudes, positions):
    tile_side = object_amplitude.shape[0]
    frame_side = probe.shape[2]
    frame_count = amplitudes.shape[0]
    object_field = jnp.stack(
        [object_amplitude * jnp.cos(object_phase), object_amplitude * jnp.sin(object_phase)]
    )
    extended = extended_2(object_field, (("row", 1), ("col", 2)), H)
    starts = positions + H
    patches = jax.vmap(
        lambda start_pair: lax.dynamic_slice(
            extended, (jnp.int32(0), start_pair[0], start_pair[1]), (2, frame_side, frame_side)
        )
    )(starts)
    forward = fourier_table(frame_side, -1.0)
    inverse = fourier_table(frame_side, 1.0)
    object_gradient, probe_gradient, weight = frame_terms(
        patches, probe, amplitudes, forward, inverse
    )
    canvas_side = tile_side + 2 * H

    def place_frame(counter, canvas):
        corner = starts[counter]
        current = lax.dynamic_slice(
            canvas, (jnp.int32(0), corner[0], corner[1]), (2, frame_side, frame_side)
        )
        return lax.dynamic_update_slice(
            canvas, current + object_gradient[counter], (jnp.int32(0), corner[0], corner[1])
        )

    canvas = lax.fori_loop(
        0, frame_count, place_frame, jnp.zeros((2, canvas_side, canvas_side), jnp.float32)
    )
    row_edges = jnp.concatenate([canvas[:, :H], canvas[:, tile_side + H :]], axis=1)
    from_rows = extended_2(row_edges, (("row", 1),), H)
    canvas = canvas.at[:, H : 2 * H].add(from_rows[:, :H])
    canvas = canvas.at[:, tile_side : tile_side + H].add(from_rows[:, 3 * H :])
    middle = canvas[:, H : tile_side + H]
    col_edges = jnp.concatenate([middle[:, :, :H], middle[:, :, tile_side + H :]], axis=2)
    from_cols = extended_2(col_edges, (("col", 2),), H)
    inner = middle[:, :, H : tile_side + H]
    inner = inner.at[:, :, :H].add(from_cols[:, :, :H])
    inner = inner.at[:, :, tile_side - H :].add(from_cols[:, :, 3 * H :])
    step_size = 1.0 / (jnp.max(jnp.sum(probe * probe, axis=(0, 1))) + 1e-06)
    new_object = object_field + inner * step_size
    total_gradient, total_weight = lax.psum((probe_gradient, weight), ("row", "col"))
    new_probe = probe + total_gradient / (total_weight + 1e-05)
    return (new_object, new_probe)


def solution(mesh):
    in_specs = (
        P("row", "col"),
        P("row", "col"),
        P(),
        P(("row", "col"), None, None),
        P(("row", "col"), None),
    )
    out_specs = (P(None, "row", "col"), P())
    return jax.shard_map(shards, mesh=mesh, in_specs=in_specs, out_specs=out_specs, check_vma=False)
```

profile of v0, /device:TPU:1, one launch (start us, length us, event | category | flops | bytes accessed | tf_op | source)
XLA Modules:
  0.0 418.9 jit_solution(17351413524869489684)
XLA Ops:
  9.9 4.0 collective-permute-start
  27.8 4.0 collective-permute-start.2
  36.5 5.9 %collective-permute-done.3 = f32[2,384,64]{2,1,0:T(8,128)S(1)} collective-permute-done((f32[2,384,64]{2,1,0:T(8,128)S(1)}, f32[2,384,64]{2,1,0:T(8,128)S(1)}, u32[]{:S(2)}, u32[]{:S(2)}) %collective-permute-start.3) | collective-permute-done | bytes 196640 | tf_op jit(solution)/shard_map/ppermute | solution.py:19
  42.8 24.2 %while.19 = (s32[]{:T(128)}, f32[2,384,384]{2,1,0:T(8,128)S(1)}, s32[8,3]{0,1:T(4,128)S(1)}, f32[8,2,256,256]{3,2,1,0:T(8,128)}, s32[]{:T(128)}) while((s32[]{:T(128)}, f32[2,384,384]{2,1,0:T(8,128)S(1)}, s32[8,3]{0,1:T(4,128)S(1)}, f32[8,2,256,256]{3,2,1,0:T(8,128)}, s32[]{:T(128)}) %tuple.90), condition=%wide.while_cond.4, body=%wide.while_body.4.sunk | while | flops 2 | bytes 1049717 | solution.py:94
  67.0 4.7 %slice_bitcast_fusion.3 = (f32[8,256,256]{2,1,0:T(8,128)}, f32[8,256,256]{2,1,0:T(8,128)}) fusion(f32[8,2,256,256]{3,2,1,0:T(8,128)} %get-tuple-element.137), kind=kLoop, calls=%fused_computation.35 | loop fusion | bytes 8388608 | tf_op jit(solution)/shard_map/mul | solution.py:53
  76.5 8.3 %multiply_subtract_fusion = (f32[8,4,1,256,256]{3,4,2,1,0:T(8,128)}, f32[8,4,1,256,256]{3,4,2,1,0:T(8,128)}) fusion(f32[8,256,256]{1,2,0:T(8,128)} %copy.50, f32[4,256,256]{1,2,0:T(8,128)} %copy.49, f32[8,256,256]{1,2,0:T(8,128)S(1)} %copy.48, f32[4,256,256]{1,2,0:T(8,128)S(1)} %copy.46), kind=kLoop, calls=%fused_computation.27 | loop fusion | flops 12582912 | bytes 23068672 | tf_op jit(solution)/shard_map/sub | solution.py:53
  84.8 19.9 %fusion = (f32[8,256,256]{1,2,0:T(8,128)}, f32[2,256,8,4,256,1]{4,1,5,3,2,0:T(8,128)}) fusion(f32[8,4,1,256,256]{3,4,2,1,0:T(8,128)} %get-tuple-element.185, f32[8,4,1,256,256]{3,4,2,1,0:T(8,128)} %get-tuple-element.184, bf16[1,256,2,256]{3,1,2,0:T(8,128)(2,1)} %get-tuple-element.201, bf16[1,256,2,256]{3,1,2,0:T(8,128)(2,1)} %get-tuple-element.202), kind=kOutput, calls=%fused_computation.10 | convolution fusion | flops 8620867584 | bytes 36175872 | tf_op jit(solution)/shard_map/fmakx,blax->fmbkl/dot_general | solution.py:38
  104.7 4.2 %maximum_divide_fusion = f32[8,256,256]{1,2,0:T(8,128)} fusion(f32[8,256,256]{1,2,0:T(8,128)} %copy.52, f32[8,256,256]{1,2,0:T(8,128)} %get-tuple-element.206), kind=kLoop, calls=%fused_computation.33 | loop fusion | flops 1048576 | bytes 6291456 | tf_op jit(solution)/shard_map/div | solution.py:60
  108.9 22.2 %bitcast_subtract_fusion = f32[8,4,2,256,256]{3,4,2,1,0:T(8,128)} fusion(f32[8,4,1,256,256]{3,4,2,1,0:T(8,128)} %get-tuple-element.185, f32[8,4,1,256,256]{3,4,2,1,0:T(8,128)} %get-tuple-element.184, bf16[1,256,2,256]{3,1,2,0:T(8,128)(2,1)} %get-tuple-element.203, bf16[1,256,2,256]{3,1,2,0:T(8,128)(2,1)} %get-tuple-element.200, ...), kind=kOutput, calls=%fused_computation.6 | convolution fusion | flops 8613003264 | bytes 52953088 | tf_op jit(solution)/shard_map/fmakx,blax->fmbkl/dot_general | solution.py:38
  131.2 11.0 %add_reduce_fusion = (f32[4,256,256]{1,2,0:T(8,128)}, f32[4,256,256]{1,2,0:T(8,128)}, f32[8,256,256]{1,2,0:T(8,128)S(1)}, f32[8,256,256]{1,2,0:T(8,128)S(1)}) fusion(f32[8,4,2,256,256]{3,4,2,1,0:T(8,128)} %bitcast_subtract_fusion, f32[8,256,256]{1,2,0:T(8,128)} %copy.50, f32[8,256,256]{1,2,0:T(8,128)S(1)} %copy.48, f32[4,256,256]{1,2,0:T(8,128)} %copy.49, ...), kind=kLoop, calls=%fused_computation.23 | loop fusion | flops 31981568 | bytes 29360128 | tf_op jit(solution)/shard_map/reduce_sum | solution.py:75
  144.5 109.0 %while.18 = (s32[]{:T(128)}, f32[2,384,384]{2,1,0:T(8,128)S(1)}, s32[8,2]{0,1:T(2,128)S(1)}, f32[8,2,256,256]{2,3,0,1:T(8,128)}, s32[]{:T(128)}, /*index=5*/s32[]{:T(128)}, s32[]{:T(128)}) while((s32[]{:T(128)}, f32[2,384,384]{2,1,0:T(8,128)S(1)}, s32[8,2]{0,1:T(2,128)S(1)}, f32[8,2,256,256]{2,3,0,1:T(8,128)}, s32[]{:T(128)}, ...), condition=%wide.region_4.5_spmd, body=%wide.region_3.4_spmd.sunk | while | flops 131080 | bytes 4718797 | solution.py:114
  150.5 7.7 %dynamic_update_slice.8 = f32[2,384,384]{2,1,0:T(8,128)S(1)} dynamic-update-slice(f32[2,384,384]{2,1,0:T(8,128)S(1)} %get-tuple-element.293, f32[2,256,256]{2,1,0:T(8,128)S(1)} %bitcast_add_fusion.2, s32[]{:T(128)} %constant.166.clone.1..sunk, s32[]{:T(128)S(6)} %select_n.100, s32[]{:T(128)S(6)} %select_n.101) | dynamic-update-slice | bytes 1048580 | tf_op jit(solution)/shard_map/while/body/eval_jaxpr/dynamic_update_slice | solution.py:110
  164.2 7.2 %dynamic_update_slice.8 = f32[2,384,384]{2,1,0:T(8,128)S(1)} dynamic-update-slice(f32[2,384,384]{2,1,0:T(8,128)S(1)} %get-tuple-element.293, f32[2,256,256]{2,1,0:T(8,128)S(1)} %bitcast_add_fusion.2, s32[]{:T(128)} %constant.166.clone.1..sunk, s32[]{:T(128)S(6)} %select_n.100, s32[]{:T(128)S(6)} %select_n.101) | dynamic-update-slice | bytes 1048580 | tf_op jit(solution)/shard_map/while/body/eval_jaxpr/dynamic_update_slice | solution.py:110
  177.4 7.1 %dynamic_update_slice.8 = f32[2,384,384]{2,1,0:T(8,128)S(1)} dynamic-update-slice(f32[2,384,384]{2,1,0:T(8,128)S(1)} %get-tuple-element.293, f32[2,256,256]{2,1,0:T(8,128)S(1)} %bitcast_add_fusion.2, s32[]{:T(128)} %constant.166.clone.1..sunk, s32[]{:T(128)S(6)} %select_n.100, s32[]{:T(128)S(6)} %select_n.101) | dynamic-update-slice | bytes 1048580 | tf_op jit(solution)/shard_map/while/body/eval_jaxpr/dynamic_update_slice | solution.py:110
  190.5 8.1 %dynamic_update_slice.8 = f32[2,384,384]{2,1,0:T(8,128)S(1)} dynamic-update-slice(f32[2,384,384]{2,1,0:T(8,128)S(1)} %get-tuple-element.293, f32[2,256,256]{2,1,0:T(8,128)S(1)} %bitcast_add_fusion.2, s32[]{:T(128)} %constant.166.clone.1..sunk, s32[]{:T(128)S(6)} %select_n.100, s32[]{:T(128)S(6)} %select_n.101) | dynamic-update-slice | bytes 1048580 | tf_op jit(solution)/shard_map/while/body/eval_jaxpr/dynamic_update_slice | solution.py:110
  204.6 7.8 %dynamic_update_slice.8 = f32[2,384,384]{2,1,0:T(8,128)S(1)} dynamic-update-slice(f32[2,384,384]{2,1,0:T(8,128)S(1)} %get-tuple-element.293, f32[2,256,256]{2,1,0:T(8,128)S(1)} %bitcast_add_fusion.2, s32[]{:T(128)} %constant.166.clone.1..sunk, s32[]{:T(128)S(6)} %select_n.100, s32[]{:T(128)S(6)} %select_n.101) | dynamic-update-slice | bytes 1048580 | tf_op jit(solution)/shard_map/while/body/eval_jaxpr/dynamic_update_slice | solution.py:110
  218.4 7.5 %dynamic_update_slice.8 = f32[2,384,384]{2,1,0:T(8,128)S(1)} dynamic-update-slice(f32[2,384,384]{2,1,0:T(8,128)S(1)} %get-tuple-element.293, f32[2,256,256]{2,1,0:T(8,128)S(1)} %bitcast_add_fusion.2, s32[]{:T(128)} %constant.166.clone.1..sunk, s32[]{:T(128)S(6)} %select_n.100, s32[]{:T(128)S(6)} %select_n.101) | dynamic-update-slice | bytes 1048580 | tf_op jit(solution)/shard_map/while/body/eval_jaxpr/dynamic_update_slice | solution.py:110
  232.0 7.7 %dynamic_update_slice.8 = f32[2,384,384]{2,1,0:T(8,128)S(1)} dynamic-update-slice(f32[2,384,384]{2,1,0:T(8,128)S(1)} %get-tuple-element.293, f32[2,256,256]{2,1,0:T(8,128)S(1)} %bitcast_add_fusion.2, s32[]{:T(128)} %constant.166.clone.1..sunk, s32[]{:T(128)S(6)} %select_n.100, s32[]{:T(128)S(6)} %select_n.101) | dynamic-update-slice | bytes 1048580 | tf_op jit(solution)/shard_map/while/body/eval_jaxpr/dynamic_update_slice | solution.py:110
  245.6 7.9 %dynamic_update_slice.8 = f32[2,384,384]{2,1,0:T(8,128)S(1)} dynamic-update-slice(f32[2,384,384]{2,1,0:T(8,128)S(1)} %get-tuple-element.293, f32[2,256,256]{2,1,0:T(8,128)S(1)} %bitcast_add_fusion.2, s32[]{:T(128)} %constant.166.clone.1..sunk, s32[]{:T(128)S(6)} %select_n.100, s32[]{:T(128)S(6)} %select_n.101) | dynamic-update-slice | bytes 1048580 | tf_op jit(solution)/shard_map/while/body/eval_jaxpr/dynamic_update_slice | solution.py:110
  260.4 3.2 multiply_reduce_fusion
  263.6 3.2 pad_maximum_fusion.2
  269.0 6.7 %collective-permute-start.6 = (f32[2,256,64]{2,1,0:T(8,128)}, f32[2,256,64]{2,1,0:T(8,128)}, u32[]{:S(2)}, u32[]{:S(2)}) collective-permute-start(f32[2,256,64]{2,1,0:T(8,128)} %get-tuple-element.191), channel_id=1, source_target_pairs={{0,1},{1,2},{2,3},{3,4},{4,5},{5,6},{6,7},{8,9},{9,10},{10,11},{11... | collective-permute-start | bytes 393224 | tf_op jit(solution)/shard_map/ppermute | solution.py:16
  283.4 4.4 %collective-permute-done.7 = f32[2,256,64]{2,1,0:T(8,128)S(1)} collective-permute-done((f32[2,256,64]{2,1,0:T(8,128)}, f32[2,256,64]{2,1,0:T(8,128)S(1)}, u32[]{:S(2)}, u32[]{:S(2)}) %collective-permute-start.7) | collective-permute-done | bytes 131104 | tf_op jit(solution)/shard_map/ppermute | solution.py:19
  290.9 115.6 %all-reduce.3.cloned.1.call-done = (f32[4,2,256,256]{2,3,0,1:T(8,128)}, f32[256,256]{1,0:T(8,128)}) async-done(((f32[4,2,256,256]{2,3,0,1:T(8,128)}, f32[256,256]{1,0:T(8,128)}), (f32[4,2,256,256]{2,3,0,1:T(8,128)}, f32[256,256]{1,0:T(8,128)})) %all-reduce.3.cloned.1.call-update) | async-done | bytes 2359312 | tf_op jit(solution)/shard_map/psum | solution.py:129
  (120 shorter events, 94.2 us)
Async XLA Ops:
  7.2 399.4 %all-reduce.3.cloned.1.call-start = ((), (), s32[]{:S(2)}) async-start(), calls=%async_computation | async-start | bytes 4718592 | tf_op jit(solution)/shard_map/psum | solution.py:129
  9.2 33.2 %copy-start.1 = (f32[1,256,256]{2,1,0:T(8,128)}, f32[1,256,256]{2,1,0:T(8,128)S(1)}, u32[]{:S(2)}) copy-start(f32[1,256,256]{2,1,0:T(8,128)S(1)} %get-tuple-element.199) | copy-start | bytes 786436
  9.9 17.6 %collective-permute-start = (f32[2,64,256]{2,1,0:T(8,128)}, f32[2,64,256]{2,1,0:T(8,128)S(1)}, u32[]{:S(2)}, u32[]{:S(2)}) collective-permute-start(f32[2,64,256]{2,1,0:T(8,128)} %get-tuple-element.196), channel_id=1, source_target_pairs={{0,8},{8,16},{16,24},{1,9},{9,17},{17,25},{2,10},{10,18},{18,26},{... | collective-permute-start | bytes 393224 | tf_op jit(solution)/shard_map/ppermute | solution.py:16
  14.0 13.6 %collective-permute-start.1 = (f32[2,64,256]{2,1,0:T(8,128)}, f32[2,64,256]{2,1,0:T(8,128)S(1)}, u32[]{:S(2)}, u32[]{:S(2)}) collective-permute-start(f32[2,64,256]{2,1,0:T(8,128)} %get-tuple-element.197), channel_id=1, source_target_pairs={{8,0},{16,8},{24,16},{9,1},{17,9},{25,17},{10,2},{18,10},{26,18},{... | collective-permute-start | bytes 393224 | tf_op jit(solution)/shard_map/ppermute | solution.py:19
  27.8 8.7 %collective-permute-start.2 = (f32[2,384,64]{2,1,0:T(8,128)S(1)}, f32[2,384,64]{2,1,0:T(8,128)S(1)}, u32[]{:S(2)}, u32[]{:S(2)}) collective-permute-start(f32[2,384,64]{2,1,0:T(8,128)S(1)} %get-tuple-element.194), channel_id=1, source_target_pairs={{0,1},{1,2},{2,3},{3,4},{4,5},{5,6},{6,7},{8,9},{9,10},{10,11},{11... | collective-permute-start | bytes 589832 | tf_op jit(solution)/shard_map/ppermute | solution.py:16
  31.8 10.6 %collective-permute-start.3 = (f32[2,384,64]{2,1,0:T(8,128)S(1)}, f32[2,384,64]{2,1,0:T(8,128)S(1)}, u32[]{:S(2)}, u32[]{:S(2)}) collective-permute-start(f32[2,384,64]{2,1,0:T(8,128)S(1)} %get-tuple-element.195), channel_id=1, source_target_pairs={{1,0},{2,1},{3,2},{4,3},{5,4},{6,5},{7,6},{9,8},{10,9},{11,10},{12... | collective-permute-start | bytes 589832 | tf_op jit(solution)/shard_map/ppermute | solution.py:19
  253.6 4.8 %collective-permute-start.4 = (f32[2,64,384]{2,1,0:T(8,128)S(1)}, f32[2,64,384]{2,1,0:T(8,128)S(1)}, u32[]{:S(2)}, u32[]{:S(2)}) collective-permute-start(f32[2,64,384]{2,1,0:T(8,128)S(1)} %slice.183), channel_id=1, source_target_pairs={{0,8},{8,16},{16,24},{1,9},{9,17},{17,25},{2,10},{10,18},{18,26},{... | collective-permute-start | bytes 589832 | tf_op jit(solution)/shard_map/ppermute | solution.py:16
  259.1 8.0 %collective-permute-start.5 = (f32[2,64,384]{2,1,0:T(8,128)}, f32[2,64,384]{2,1,0:T(8,128)}, u32[]{:S(2)}, u32[]{:S(2)}) collective-permute-start(f32[2,64,384]{2,1,0:T(8,128)} %get-tuple-element.192), channel_id=1, source_target_pairs={{8,0},{16,8},{24,16},{9,1},{17,9},{25,17},{10,2},{18,10},{26,18},{... | collective-permute-start | bytes 589832 | tf_op jit(solution)/shard_map/ppermute | solution.py:19
  263.6 12.1 %copy-start = (f32[4,2,256,256]{3,2,1,0:T(8,128)S(1)}, f32[4,2,256,256]{3,2,1,0:T(8,128)}, u32[]{:S(2)}) copy-start(f32[4,2,256,256]{3,2,1,0:T(8,128)} %param.17) | copy-start | bytes 6291460
  269.0 12.2 %collective-permute-start.6 = (f32[2,256,64]{2,1,0:T(8,128)}, f32[2,256,64]{2,1,0:T(8,128)}, u32[]{:S(2)}, u32[]{:S(2)}) collective-permute-start(f32[2,256,64]{2,1,0:T(8,128)} %get-tuple-element.191), channel_id=1, source_target_pairs={{0,1},{1,2},{2,3},{3,4},{4,5},{5,6},{6,7},{8,9},{9,10},{10,11},{11... | collective-permute-start | bytes 393224 | tf_op jit(solution)/shard_map/ppermute | solution.py:16
  279.2 8.5 %collective-permute-start.7 = (f32[2,256,64]{2,1,0:T(8,128)}, f32[2,256,64]{2,1,0:T(8,128)S(1)}, u32[]{:S(2)}, u32[]{:S(2)}) collective-permute-start(f32[2,256,64]{2,1,0:T(8,128)} %get-tuple-element.190), channel_id=1, source_target_pairs={{1,0},{2,1},{3,2},{4,3},{5,4},{6,5},{7,6},{9,8},{10,9},{11,10},{12... | collective-permute-start | bytes 393224 | tf_op jit(solution)/shard_map/ppermute | solution.py:19
Sparse Core Ops, SparseCore 0:
  267.0 139.5 all-reduce.2
where the time goes:
time: 422 us; the launch traced here: 419 us
  waiting for transfers between devices  128 us (30%)
  local copies, waits for them, and re-layouts  127 us (30%)
  other arithmetic  52.8 us (13%)
  matrix products  42.1 us (10%)
  loops' own time  31.4 us (7%)
  starting transfers between devices  23.2 us (5%)
  between operations  15 us (4%)
    psum x1, waiting for transfers between devices, shards(): lax.psum((probe_gradient, weight), ('row', 'col'))  116 us
    dynamic_update_slice x8, local copies, waits for them, and re-layouts, place_frame(): lax.dynamic_update_slice(canvas, current + object_gradient[counter], (jnp...  60.9 us
    dot_general x2, matrix products, transform(): jnp.einsum('fmakx,blax->fmbkl', halfway.astype(jnp.bfloat16), matrix, pre...  42.1 us
    another operation x1, loops' own time, shards(): lax.fori_loop(0, frame_count, place_frame, jnp.zeros((2, canvas_side, can...  31.4 us
    gather x24, local copies, waits for them, and re-layouts  24.2 us
    ppermute x4, starting transfers between devices, extended_2(): lax.ppermute(lax.slice_in_dim(block, block.shape[dim] - width, None, axis...  16.6 us
    reduce_sum x1, other arithmetic, frame_terms(): jnp.sum(object_real * change_real + object_imag * change_imag, axis=0)  11 us
    ppermute x4, waiting for transfers between devices, extended_2(): lax.ppermute(lax.slice_in_dim(block, 0, width, axis=dim), axis, backward)  10.5 us
  transfers between devices with their start and end apart: 9, of which 5 were waited for; matrix products, arithmetic and copies ran while one was open for 8% of the time, Pallas kernels for 0%

commit v1 on v0

v1 whole, which is shorter than its diff:
```python
import math

import jax
import jax.numpy as jnp
from jax import lax
from jax.experimental import pallas as pl
from jax.experimental.pallas import tpu as pltpu
from jax.sharding import PartitionSpec as P

H = 64


def extended_2(block, sides, width):
    for axis, dim in sides:
        count = lax.axis_size(axis)
        forward = [(i, i + 1) for i in range(count - 1)]
        backward = [(target, source) for source, target in forward]
        low = lax.ppermute(
            lax.slice_in_dim(block, block.shape[dim] - width, None, axis=dim), axis, forward
        )
        high = lax.ppermute(lax.slice_in_dim(block, 0, width, axis=dim), axis, backward)
        block = jnp.concatenate([low, block, high], axis=dim)
    return block


def fourier_tables(side, sign):
    counter = jnp.arange(side, dtype=jnp.int32)
    product = counter[:, None] * counter[None, :] % side
    angle = product.astype(jnp.float32) * (2.0 * math.pi / side)
    norming = 1.0 / math.sqrt(side)
    real = (jnp.cos(angle) * norming).astype(jnp.bfloat16)
    imag = (sign * jnp.sin(angle) * norming).astype(jnp.bfloat16)
    left = jnp.concatenate(
        [jnp.concatenate([real, -imag], axis=1), jnp.concatenate([imag, real], axis=1)], axis=0
    )
    right = jnp.concatenate(
        [jnp.concatenate([real, imag], axis=1), jnp.concatenate([-imag, real], axis=1)], axis=0
    )
    return left, right


def dot(a, b):
    return jnp.dot(a, b, preferred_element_type=jnp.float32)


def frames_kernel(
    pos_ref, ext_ref, probe_ref, amp_ref, fl_ref, fr_ref, il_ref, ir_ref,
    canvas_ref, s_ref, w_ref,
    o_scr, x_scr, h_scr, spec_scr, int_scr, p2_scr, g_scr,
):
    frame = pl.program_id(0)
    modes, _, n, _ = probe_ref.shape
    wide = ext_ref.shape[2]
    step = 32
    chunks = [pl.ds(r, step) for r in range(0, n, step)]
    low = [pl.ds(n + r, step) for r in range(0, n, step)]

    @pl.when(frame == 0)
    def _():
        canvas_ref[...] = jnp.zeros_like(canvas_ref)
        s_ref[...] = jnp.zeros_like(s_ref)
        w_ref[...] = jnp.zeros_like(w_ref)
        for rows in chunks:
            total = jnp.zeros((step, n), jnp.float32)
            for m in range(modes):
                for c in range(2):
                    total += probe_ref[m, c, rows, :] * probe_ref[m, c, rows, :]
            p2_scr[rows, :] = total

    r0 = pos_ref[frame, 0] + H
    c0 = pos_ref[frame, 1] + H
    base = pl.multiple_of(r0 // 8 * 8, 8)
    off = r0 - base
    tall = 64
    for r in range(0, n, tall):
        rows = pl.ds(r, tall)
        weight = w_ref[rows, :]
        for c in range(2):
            part = ext_ref[c, pl.ds(base + r, tall + 8), :]
            part = pltpu.roll(part, lax.rem(wide - c0, wide), axis=1)[:, :n]
            part = pltpu.roll(part, lax.rem(tall + 8 - off, tall + 8), axis=0)[:tall]
            o_scr[c, rows, :] = part
            weight += part * part
        w_ref[rows, :] = weight

    for m in range(modes):
        for rows, under in zip(chunks, low):
            pr, pi = probe_ref[m, 0, rows, :], probe_ref[m, 1, rows, :]
            o_r, o_i = o_scr[0, rows, :], o_scr[1, rows, :]
            x_scr[m, rows, :] = (pr * o_r - pi * o_i).astype(jnp.bfloat16)
            x_scr[m, under, :] = (pr * o_i + pi * o_r).astype(jnp.bfloat16)
        half = dot(fl_ref[...], x_scr[m]).astype(jnp.bfloat16)
        h_scr[m, :, :n] = half[:n]
        h_scr[m, :, n:] = half[n:]
        spec_scr[m] = dot(h_scr[m], fr_ref[...])

    for rows in chunks:
        total = jnp.zeros((step, n), jnp.float32)
        for m in range(modes):
            a, b = spec_scr[m, rows, :n], spec_scr[m, rows, n:]
            total += a * a + b * b
        int_scr[rows, :] = amp_ref[0, rows, :] / jnp.maximum(jnp.sqrt(total), 1.0)

    for m in range(modes):
        for rows, under in zip(chunks, low):
            fac = int_scr[rows, :]
            x_scr[m, rows, :] = (spec_scr[m, rows, :n] * fac).astype(jnp.bfloat16)
            x_scr[m, under, :] = (spec_scr[m, rows, n:] * fac).astype(jnp.bfloat16)
        half = dot(il_ref[...], x_scr[m]).astype(jnp.bfloat16)
        h_scr[m, :, :n] = half[:n]
        h_scr[m, :, n:] = half[n:]
        spec_scr[m] = dot(h_scr[m], ir_ref[...])
        for rows in chunks:
            br, bi = spec_scr[m, rows, :n], spec_scr[m, rows, n:]
            o_r, o_i = o_scr[0, rows, :], o_scr[1, rows, :]
            pr, pi = probe_ref[m, 0, rows, :], probe_ref[m, 1, rows, :]
            s_ref[m, 0, rows, :] += o_r * br + o_i * bi
            s_ref[m, 1, rows, :] += o_r * bi - o_i * br
            gr = pr * br + pi * bi
            gi = pr * bi - pi * br
            if m == 0:
                p2 = p2_scr[rows, :]
                gr -= o_r * p2
                gi -= o_i * p2
            else:
                gr += g_scr[0, rows, :]
                gi += g_scr[1, rows, :]
            g_scr[0, rows, :] = gr
            g_scr[1, rows, :] = gi

    for r in range(0, n, tall):
        for c in range(2):
            part = jnp.concatenate(
                [g_scr[c, pl.ds(r, tall), :], jnp.zeros((8, n), jnp.float32)], axis=0
            )
            part = pltpu.roll(part, off, axis=0)
            part = jnp.concatenate([part, jnp.zeros((tall + 8, wide - n), jnp.float32)], axis=1)
            canvas_ref[c, pl.ds(base + r, tall + 8), :] += pltpu.roll(part, c0, axis=1)


def frame_terms(positions, extended, probe, amplitudes):
    modes, _, n, _ = probe.shape
    frames = amplitudes.shape[0]
    wide = extended.shape[2]
    high = extended.shape[1]
    forward = fourier_tables(n, -1.0)
    inverse = fourier_tables(n, 1.0)
    f32 = jnp.float32

    def whole(shape):
        return pl.BlockSpec(shape, lambda i, pos: (0,) * len(shape))

    return pl.pallas_call(
        frames_kernel,
        grid_spec=pltpu.PrefetchScalarGridSpec(
            num_scalar_prefetch=1,
            grid=(frames,),
            in_specs=[
                whole(extended.shape),
                whole(probe.shape),
                pl.BlockSpec((1, n, n), lambda i, pos: (i, 0, 0)),
            ]
            + [whole((2 * n, 2 * n))] * 4,
            out_specs=[whole((2, high, wide)), whole(probe.shape), whole((n, n))],
            scratch_shapes=[
                pltpu.VMEM((2, n, n), f32),
                pltpu.VMEM((modes, 2 * n, n), jnp.bfloat16),
                pltpu.VMEM((modes, n, 2 * n), jnp.bfloat16),
                pltpu.VMEM((modes, n, 2 * n), f32),
                pltpu.VMEM((n, n), f32),
                pltpu.VMEM((n, n), f32),
                pltpu.VMEM((2, n, n), f32),
            ],
        ),
        out_shape=[
            jax.ShapeDtypeStruct((2, high, wide), f32),
            jax.ShapeDtypeStruct(probe.shape, f32),
            jax.ShapeDtypeStruct((n, n), f32),
        ],
        compiler_params=pltpu.CompilerParams(vmem_limit_bytes=48 * 1024 * 1024),
        name="frames",
    )(positions, extended, probe, amplitudes, *forward, *inverse)


def shards(object_amplitude, object_phase, probe, amplitudes, positions):
    tile_side = object_amplitude.shape[0]
    object_field = jnp.stack(
        [object_amplitude * jnp.cos(object_phase), object_amplitude * jnp.sin(object_phase)]
    )
    extended = extended_2(object_field, (("row", 1), ("col", 2)), H)
    extended = jnp.pad(extended, ((0, 0), (0, 8), (0, 0)))
    canvas, probe_sum, weight = frame_terms(positions, extended, probe, amplitudes)
    canvas = canvas[:, : tile_side + 2 * H]
    row_edges = jnp.concatenate([canvas[:, :H], canvas[:, tile_side + H :]], axis=1)
    from_rows = extended_2(row_edges, (("row", 1),), H)
    canvas = canvas.at[:, H : 2 * H].add(from_rows[:, :H])
    canvas = canvas.at[:, tile_side : tile_side + H].add(from_rows[:, 3 * H :])
    middle = canvas[:, H : tile_side + H]
    col_edges = jnp.concatenate([middle[:, :, :H], middle[:, :, tile_side + H :]], axis=2)
    from_cols = extended_2(col_edges, (("col", 2),), H)
    inner = middle[:, :, H : tile_side + H]
    inner = inner.at[:, :, :H].add(from_cols[:, :, :H])
    inner = inner.at[:, :, tile_side - H :].add(from_cols[:, :, 3 * H :])
    step_size = 1.0 / (jnp.max(jnp.sum(probe * probe, axis=(0, 1))) + 1e-06)
    new_object = object_field + inner * step_size
    total_sum, total_weight = lax.psum((probe_sum, weight), ("row", "col"))
    new_probe = probe + (total_sum - probe * total_weight) / (total_weight + 1e-05)
    return (new_object, new_probe)


def solution(mesh):
    in_specs = (
        P("row", "col"),
        P("row", "col"),
        P(),
        P(("row", "col"), None, None),
        P(("row", "col"), None),
    )
    out_specs = (P(None, "row", "col"), P())
    return jax.shard_map(shards, mesh=mesh, in_specs=in_specs, out_specs=out_specs, check_vma=False)
```

time: 422 us -> 228 us (0.54)
  local copies, waits for them, and re-layouts: 127 us -> 5.03 us
  matrix products: 42.1 us -> 0 us
  other arithmetic: 52.8 us -> 13.6 us
  Pallas kernels: 0 us -> 37.4 us
  loops' own time: 31.4 us -> 0 us
    dynamic_update_slice x8 -> x0, local copies, waits for them, and re-layouts: 60.9 us -> none  [place_frame(): lax.dynamic_update_slice(canvas, current + object_gradient[counter], (jnp...]
    dot_general x2 -> x0, matrix products: 42.1 us -> none  [transform(): jnp.einsum('fmakx,blax->fmbkl', halfway.astype(jnp.bfloat16), matrix, pre...]
    pallas_call x0 -> x1, Pallas kernels: none -> 37.4 us  [frame_terms(): pl.pallas_call(frames_kernel, grid_spec=pltpu.PrefetchScalarGridSpec(num_...]
    another operation x2 -> x0, loops' own time: 31.4 us -> none  [the longest x1 31.4 us: shards(): lax.fori_loop(0, frame_count, place_frame, jnp.zeros((2, canvas_side, can...]
    gather x24 -> x0, local copies, waits for them, and re-layouts: 24.2 us -> none
    reduce_sum x3 -> x0, other arithmetic: 15.1 us -> none  [the longest x1 11 us: frame_terms(): jnp.sum(object_real * change_real + object_imag * change_imag, axis=0)]
    mul x6 -> x0, local copies, waits for them, and re-layouts: 15.1 us -> none  [the longest x2 6.58 us: frame_terms(): probe_real * object_real - probe_imag * object_imag]
    dynamic_slice x24 -> x0, local copies, waits for them, and re-layouts: 10.9 us -> none  [the longest x16 10.3 us: place_frame(): object_gradient[counter]]
  transfers between devices with their start and end apart: 9 -> 9, of which waited for: 5 -> 8; matrix products, arithmetic and copies ran while one was open for 8% -> 4% of each run, Pallas kernels for 0% -> 0%
where the time goes in v1:
time: 228 us; the launch traced here: 226 us
  waiting for transfers between devices  132 us (58%)
  Pallas kernels  37.4 us (16%)
  starting transfers between devices  23.6 us (10%)
  between operations  14.9 us (7%)
  other arithmetic  13.6 us (6%)
  local copies, waits for them, and re-layouts  5.03 us (2%)
    psum x1, waiting for transfers between devices, shards(): total_sum, total_weight = lax.psum((probe_sum, weight), ('row', 'col'))  112 us
    pallas_call x1, Pallas kernels, frame_terms(): pl.pallas_call(frames_kernel, grid_spec=pltpu.PrefetchScalarGridSpec(num_...  37.4 us
    ppermute x4, starting transfers between devices, extended_2(): lax.ppermute(lax.slice_in_dim(block, block.shape[dim] - width, None, axis...  17.1 us
    ppermute x4, waiting for transfers between devices, extended_2(): lax.ppermute(lax.slice_in_dim(block, 0, width, axis=dim), axis, backward)  15.1 us
    ppermute x4, starting transfers between devices, extended_2(): lax.ppermute(lax.slice_in_dim(block, 0, width, axis=dim), axis, backward)  6.43 us
    ppermute x4, waiting for transfers between devices, extended_2(): lax.ppermute(lax.slice_in_dim(block, block.shape[dim] - width, None, axis...  4.57 us
  transfers between devices with their start and end apart: 9, of which 8 were waited for; matrix products, arithmetic and copies ran while one was open for 4% of the time, Pallas kernels for 0%

profile of v1, /device:TPU:1, one launch (start us, length us, event | category | flops | bytes accessed | tf_op | source)
XLA Modules:
  0.0 226.1 jit_solution(7020272124273234204)
XLA Ops:
  7.2 1.9 multiply_bitcast_fusion.1
  9.2 4.0 %collective-permute-start = (f32[2,64,256]{2,1,0:T(8,128)S(1)}, f32[2,64,256]{2,1,0:T(8,128)S(1)}, u32[]{:S(2)}, u32[]{:S(2)}) collective-permute-start(f32[2,64,256]{2,1,0:T(8,128)S(1)} %get-tuple-element.66), channel_id=1, source_target_pairs={{0,8},{8,16},{16,24},{1,9},{9,17},{17,25},{2,10},{10,18},{18,26},{... | collective-permute-start | bytes 393224 | tf_op jit(solution)/shard_map/ppermute | solution.py:18
  13.2 1.3 collective-permute-start.1
  14.5 1.0 fusion.22
  15.5 1.0 multiply_convert_fusion
  16.6 2.4 %collective-permute-done.1 = f32[2,64,256]{2,1,0:T(8,128)S(1)} collective-permute-done((f32[2,64,256]{2,1,0:T(8,128)S(1)}, f32[2,64,256]{2,1,0:T(8,128)S(1)}, u32[]{:S(2)}, u32[]{:S(2)}) %collective-permute-start.1) | collective-permute-done | bytes 131104 | tf_op jit(solution)/shard_map/ppermute | solution.py:21
  19.2 5.1 %collective-permute-start.2 = (f32[2,384,64]{2,1,0:T(8,128)S(1)}, f32[2,384,64]{2,1,0:T(8,128)S(1)}, u32[]{:S(2)}, u32[]{:S(2)}) collective-permute-start(f32[2,384,64]{2,1,0:T(8,128)S(1)} %get-tuple-element.64), channel_id=1, source_target_pairs={{0,1},{1,2},{2,3},{3,4},{4,5},{5,6},{6,7},{8,9},{9,10},{10,11},{11... | collective-permute-start | bytes 589832 | tf_op jit(solution)/shard_map/ppermute | solution.py:18
  24.3 1.9 collective-permute-start.3
  27.5 1.5 collective-permute-done.2
  29.0 5.9 %collective-permute-done.3 = f32[2,384,64]{2,1,0:T(8,128)S(1)} collective-permute-done((f32[2,384,64]{2,1,0:T(8,128)S(1)}, f32[2,384,64]{2,1,0:T(8,128)S(1)}, u32[]{:S(2)}, u32[]{:S(2)}) %collective-permute-start.3) | collective-permute-done | bytes 196640 | tf_op jit(solution)/shard_map/ppermute | solution.py:21
  35.3 37.4 %frames.1 = (f32[2,392,384]{2,1,0:T(8,128)S(1)}, f32[4,2,256,256]{3,2,1,0:T(8,128)}, f32[256,256]{1,0:T(8,128)}) custom-call(s32[8,2]{1,0:T(8,128)S(1)} %copy.8.pos_ref, f32[2,392,384]{2,1,0:T(8,128)S(1)} %select_maximum_fusion.ext_ref, f32[4,2,256,256]{3,2,1,0:T(8,128)} %probe_ref.1, f32[8,256,256]{2,1,0:T(8,128)} %amp_ref.1, ...), custom_call_target="tpu_custom_call" | custom-call | tf_op jit(solution)/shard_map/frames/pallas_call | solution.py:153
  73.5 3.2 %collective-permute-start.4 = (f32[2,64,384]{2,1,0:T(8,128)}, f32[2,64,384]{2,1,0:T(8,128)S(1)}, u32[]{:S(2)}, u32[]{:S(2)}) collective-permute-start(f32[2,64,384]{2,1,0:T(8,128)} %get-tuple-element.61), channel_id=1, source_target_pairs={{0,8},{8,16},{16,24},{1,9},{9,17},{17,25},{2,10},{10,18},{18,26},{... | collective-permute-start | bytes 589832 | tf_op jit(solution)/shard_map/ppermute | solution.py:18
  76.8 1.3 collective-permute-start.5
  78.2 1.5 collective-permute-done.4
  79.7 3.6 %collective-permute-done.5 = f32[2,64,384]{2,1,0:T(8,128)S(1)} collective-permute-done((f32[2,64,384]{2,1,0:T(8,128)S(1)}, f32[2,64,384]{2,1,0:T(8,128)S(1)}, u32[]{:S(2)}, u32[]{:S(2)}) %collective-permute-start.5) | collective-permute-done | bytes 196640 | tf_op jit(solution)/shard_map/ppermute | solution.py:21
  84.1 4.7 %collective-permute-start.6 = (f32[2,256,64]{2,1,0:T(8,128)S(1)}, f32[2,256,64]{2,1,0:T(8,128)S(1)}, u32[]{:S(2)}, u32[]{:S(2)}) collective-permute-start(f32[2,256,64]{2,1,0:T(8,128)S(1)} %get-tuple-element.63), channel_id=1, source_target_pairs={{0,1},{1,2},{2,3},{3,4},{4,5},{5,6},{6,7},{8,9},{9,10},{10,11},{11... | collective-permute-start | bytes 393224 | tf_op jit(solution)/shard_map/ppermute | solution.py:18
  89.0 1.9 collective-permute-start.7
  90.9 1.6 collective-permute-done.6
  93.3 1.8 scatter-add.16
  95.2 3.2 %collective-permute-done.7 = f32[2,256,64]{2,1,0:T(8,128)} collective-permute-done((f32[2,256,64]{2,1,0:T(8,128)}, f32[2,256,64]{2,1,0:T(8,128)}, u32[]{:S(2)}, u32[]{:S(2)}) %collective-permute-start.7) | collective-permute-done | bytes 131104 | tf_op jit(solution)/shard_map/ppermute | solution.py:21
  98.4 1.1 slice_add_fusion
  99.5 1.2 scatter-add.19
  100.7 112.0 %all-reduce.4.cloned.1.call-done = (f32[4,2,256,256]{3,2,1,0:T(8,128)}, f32[256,256]{1,0:T(8,128)}) async-done(((f32[4,2,256,256]{3,2,1,0:T(8,128)}, f32[256,256]{1,0:T(8,128)}), (f32[4,2,256,256]{3,2,1,0:T(8,128)}, f32[256,256]{1,0:T(8,128)})) %all-reduce.4.cloned.1.call-update) | async-done | bytes 2359312 | tf_op jit(solution)/shard_map/psum | solution.py:206
  213.7 3.4 %divide_add_fusion = (f32[4,2,256,256]{3,2,1,0:T(8,128)}, f32[256,256]{1,0:T(8,128)S(1)}) fusion(f32[4,2,256,256]{3,2,1,0:T(8,128)S(1)} %copy-done, f32[4,2,256,256]{3,2,1,0:T(8,128)} %get-tuple-element.56, f32[256,256]{1,0:T(8,128)S(1)} %broadcast_add_fusion, f32[256,256]{1,0:T(8,128)} %get-tuple-element.57), kind=kLoop, calls=%fused_computation | loop fusion | flops 3080192 | bytes 7077888 | tf_op jit(solution)/shard_map/add | solution.py:207
  (24 shorter events, 7.2 us)
Async XLA Ops:
  7.2 205.5 %all-reduce.4.cloned.1.call-start = ((), (), s32[]{:S(2)}) async-start(), calls=%async_computation | async-start | bytes 4718592 | tf_op jit(solution)/shard_map/psum | solution.py:206
  9.2 7.4 %collective-permute-start = (f32[2,64,256]{2,1,0:T(8,128)S(1)}, f32[2,64,256]{2,1,0:T(8,128)S(1)}, u32[]{:S(2)}, u32[]{:S(2)}) collective-permute-start(f32[2,64,256]{2,1,0:T(8,128)S(1)} %get-tuple-element.66), channel_id=1, source_target_pairs={{0,8},{8,16},{16,24},{1,9},{9,17},{17,25},{2,10},{10,18},{18,26},{... | collective-permute-start | bytes 393224 | tf_op jit(solution)/shard_map/ppermute | solution.py:18
  13.2 5.7 %collective-permute-start.1 = (f32[2,64,256]{2,1,0:T(8,128)S(1)}, f32[2,64,256]{2,1,0:T(8,128)S(1)}, u32[]{:S(2)}, u32[]{:S(2)}) collective-permute-start(f32[2,64,256]{2,1,0:T(8,128)S(1)} %get-tuple-element.67), channel_id=1, source_target_pairs={{8,0},{16,8},{24,16},{9,1},{17,9},{25,17},{10,2},{18,10},{26,18},{... | collective-permute-start | bytes 393224 | tf_op jit(solution)/shard_map/ppermute | solution.py:21
  19.0 8.2 %copy-start.1 = (s32[8,2]{0,1:T(2,128)S(1)}, s32[8,2]{0,1:T(2,128)}, u32[]{:S(2)}) copy-start(s32[8,2]{0,1:T(2,128)} %param.17) | copy-start | bytes 196
  19.2 9.8 %collective-permute-start.2 = (f32[2,384,64]{2,1,0:T(8,128)S(1)}, f32[2,384,64]{2,1,0:T(8,128)S(1)}, u32[]{:S(2)}, u32[]{:S(2)}) collective-permute-start(f32[2,384,64]{2,1,0:T(8,128)S(1)} %get-tuple-element.64), channel_id=1, source_target_pairs={{0,1},{1,2},{2,3},{3,4},{4,5},{5,6},{6,7},{8,9},{9,10},{10,11},{11... | collective-permute-start | bytes 589832 | tf_op jit(solution)/shard_map/ppermute | solution.py:18
  24.3 10.6 %collective-permute-start.3 = (f32[2,384,64]{2,1,0:T(8,128)S(1)}, f32[2,384,64]{2,1,0:T(8,128)S(1)}, u32[]{:S(2)}, u32[]{:S(2)}) collective-permute-start(f32[2,384,64]{2,1,0:T(8,128)S(1)} %get-tuple-element.65), channel_id=1, source_target_pairs={{1,0},{2,1},{3,2},{4,3},{5,4},{6,5},{7,6},{9,8},{10,9},{11,10},{12... | collective-permute-start | bytes 589832 | tf_op jit(solution)/shard_map/ppermute | solution.py:21
  73.5 6.2 %collective-permute-start.4 = (f32[2,64,384]{2,1,0:T(8,128)}, f32[2,64,384]{2,1,0:T(8,128)S(1)}, u32[]{:S(2)}, u32[]{:S(2)}) collective-permute-start(f32[2,64,384]{2,1,0:T(8,128)} %get-tuple-element.61), channel_id=1, source_target_pairs={{0,8},{8,16},{16,24},{1,9},{9,17},{17,25},{2,10},{10,18},{18,26},{... | collective-permute-start | bytes 589832 | tf_op jit(solution)/shard_map/ppermute | solution.py:18
  76.8 6.4 %collective-permute-start.5 = (f32[2,64,384]{2,1,0:T(8,128)S(1)}, f32[2,64,384]{2,1,0:T(8,128)S(1)}, u32[]{:S(2)}, u32[]{:S(2)}) collective-permute-start(f32[2,64,384]{2,1,0:T(8,128)S(1)} %get-tuple-element.60), channel_id=1, source_target_pairs={{8,0},{16,8},{24,16},{9,1},{17,9},{25,17},{10,2},{18,10},{26,18},{... | collective-permute-start | bytes 589832 | tf_op jit(solution)/shard_map/ppermute | solution.py:21
  84.1 8.4 %collective-permute-start.6 = (f32[2,256,64]{2,1,0:T(8,128)S(1)}, f32[2,256,64]{2,1,0:T(8,128)S(1)}, u32[]{:S(2)}, u32[]{:S(2)}) collective-permute-start(f32[2,256,64]{2,1,0:T(8,128)S(1)} %get-tuple-element.63), channel_id=1, source_target_pairs={{0,1},{1,2},{2,3},{3,4},{4,5},{5,6},{6,7},{8,9},{9,10},{10,11},{11... | collective-permute-start | bytes 393224 | tf_op jit(solution)/shard_map/ppermute | solution.py:18
  89.0 9.4 %collective-permute-start.7 = (f32[2,256,64]{2,1,0:T(8,128)}, f32[2,256,64]{2,1,0:T(8,128)}, u32[]{:S(2)}, u32[]{:S(2)}) collective-permute-start(f32[2,256,64]{2,1,0:T(8,128)} %get-tuple-element.62), channel_id=1, source_target_pairs={{1,0},{2,1},{3,2},{4,3},{5,4},{6,5},{7,6},{9,8},{10,9},{11,10},{12... | collective-permute-start | bytes 393224 | tf_op jit(solution)/shard_map/ppermute | solution.py:21
  93.3 120.3 %copy-start = (f32[4,2,256,256]{3,2,1,0:T(8,128)S(1)}, f32[4,2,256,256]{3,2,1,0:T(8,128)}, u32[]{:S(2)}) copy-start(f32[4,2,256,256]{3,2,1,0:T(8,128)} %probe_ref.1) | copy-start | bytes 6291460
Sparse Core Ops, SparseCore 0:
  78.3 134.3 all-reduce.3

commit v2 on v1

--- a/solution.py
+++ b/solution.py
@@ -1,3 +1,4 @@
+import functools
 import math
 
 import jax
@@ -45,13 +46,20 @@
 
 def frames_kernel(
     pos_ref, ext_ref, probe_ref, amp_ref, fl_ref, fr_ref, il_ref, ir_ref,
-    canvas_ref, s_ref, w_ref,
+    canvas_ref, s_ref,
     o_scr, x_scr, h_scr, spec_scr, int_scr, p2_scr, g_scr,
 ):
     frame = pl.program_id(0)
     modes, _, n, _ = probe_ref.shape
     wide = ext_ref.shape[2]
     step = 32
+    lanes = n // 2
+    planes = 2 * modes
+
+    def add_sum(plane, rows, value):
+        s_ref[0, plane, rows, :] += value[:, :lanes]
+        s_ref[1, plane, rows, :] += value[:, lanes:]
+
     chunks = [pl.ds(r, step) for r in range(0, n, step)]
     low = [pl.ds(n + r, step) for r in range(0, n, step)]
 
@@ -59,7 +67,6 @@
     def _():
         canvas_ref[...] = jnp.zeros_like(canvas_ref)
         s_ref[...] = jnp.zeros_like(s_ref)
-        w_ref[...] = jnp.zeros_like(w_ref)
         for rows in chunks:
             total = jnp.zeros((step, n), jnp.float32)
             for m in range(modes):
@@ -74,14 +81,14 @@
     tall = 64
     for r in range(0, n, tall):
         rows = pl.ds(r, tall)
-        weight = w_ref[rows, :]
+        weight = jnp.zeros((tall, n), jnp.float32)
         for c in range(2):
             part = ext_ref[c, pl.ds(base + r, tall + 8), :]
             part = pltpu.roll(part, lax.rem(wide - c0, wide), axis=1)[:, :n]
             part = pltpu.roll(part, lax.rem(tall + 8 - off, tall + 8), axis=0)[:tall]
             o_scr[c, rows, :] = part
             weight += part * part
-        w_ref[rows, :] = weight
+        add_sum(planes, rows, weight)
 
     for m in range(modes):
         for rows, under in zip(chunks, low):
@@ -114,8 +121,8 @@
             br, bi = spec_scr[m, rows, :n], spec_scr[m, rows, n:]
             o_r, o_i = o_scr[0, rows, :], o_scr[1, rows, :]
             pr, pi = probe_ref[m, 0, rows, :], probe_ref[m, 1, rows, :]
-            s_ref[m, 0, rows, :] += o_r * br + o_i * bi
-            s_ref[m, 1, rows, :] += o_r * bi - o_i * br
+            add_sum(2 * m, rows, o_r * br + o_i * bi)
+            add_sum(2 * m + 1, rows, o_r * bi - o_i * br)
             gr = pr * br + pi * bi
             gi = pr * bi - pi * br
             if m == 0:
@@ -146,6 +153,7 @@
     forward = fourier_tables(n, -1.0)
     inverse = fourier_tables(n, 1.0)
     f32 = jnp.float32
+    sums = (2, 2 * modes + 1, n, n // 2)
 
     def whole(shape):
         return pl.BlockSpec(shape, lambda i, pos: (0,) * len(shape))
@@ -161,7 +169,7 @@
                 pl.BlockSpec((1, n, n), lambda i, pos: (i, 0, 0)),
             ]
             + [whole((2 * n, 2 * n))] * 4,
-            out_specs=[whole((2, high, wide)), whole(probe.shape), whole((n, n))],
+            out_specs=[whole((2, high, wide)), whole(sums)],
             scratch_shapes=[
                 pltpu.VMEM((2, n, n), f32),
                 pltpu.VMEM((modes, 2 * n, n), jnp.bfloat16),
@@ -174,12 +182,137 @@
         ),
         out_shape=[
             jax.ShapeDtypeStruct((2, high, wide), f32),
-            jax.ShapeDtypeStruct(probe.shape, f32),
-            jax.ShapeDtypeStruct((n, n), f32),
+            jax.ShapeDtypeStruct(sums, f32),
         ],
         compiler_params=pltpu.CompilerParams(vmem_limit_bytes=48 * 1024 * 1024),
         name="frames",
     )(positions, extended, probe, amplitudes, *forward, *inverse)
+
+
+def plan(sizes, rows):
+    bits = [[(axis, b) for b in range(size.bit_length() - 1)] for axis, size in sizes]
+    row_bits, col_bits = bits
+    rest = col_bits[1:]
+    cut = len(rest) // 2
+    orders = [col_bits[:1] + rest + row_bits, col_bits[:1] + rest[cut:] + rest[:cut] + row_bits]
+    plans = []
+    for order in orders:
+        left, stages, offset = rows, [], 0
+        for axis, bit in order:
+            halved = left > 8
+            left = left // 2 if halved else left
+            stages.append((axis, bit, halved, left, offset))
+            offset += left
+        plans.append(stages)
+    return plans, max(stages[-1][3] + stages[-1][4] for stages in plans)
+
+
+def total_kernel(plans, in_ref, out_ref, partial, landed, send_rs, recv_rs, send_ag, recv_ag):
+    coords = {"row": lax.axis_index("row"), "col": lax.axis_index("col")}
+
+    def bit_of(axis, bit):
+        return lax.rem(coords[axis] // (1 << bit), 2)
+
+    def partner(axis, bit):
+        flipped = dict(coords)
+        flipped[axis] = coords[axis] + (1 - 2 * bit_of(axis, bit)) * (1 << bit)
+        return (flipped["row"], flipped["col"])
+
+    barrier = pltpu.get_barrier_semaphore()
+    for axis, bit, *_ in plans[0]:
+        pl.semaphore_signal(
+            barrier, inc=1, device_id=partner(axis, bit), device_id_type=pl.DeviceIdType.MESH
+        )
+    pl.semaphore_wait(barrier, len(plans[0]))
+
+    count = len(plans[0])
+    starts = [[0], [0]]
+    flights = [None, None]
+
+    def send(part, stage):
+        axis, bit, halved, size, offset = plans[part][stage]
+        start = starts[part][-1]
+        mine = bit_of(axis, bit)
+        source = in_ref if stage == 0 else partial
+        gone = pl.multiple_of(start + (1 - mine) * size, 8) if halved else start
+        kept = pl.multiple_of(start + mine * size, 8) if halved else start
+        starts[part].append(kept)
+        copy = pltpu.make_async_remote_copy(
+            src_ref=source.at[part, :, pl.ds(gone, size), :],
+            dst_ref=landed.at[part, :, pl.ds(offset, size), :],
+            send_sem=send_rs.at[part, stage],
+            recv_sem=recv_rs.at[part, stage],
+            device_id=partner(axis, bit),
+            device_id_type=pl.DeviceIdType.MESH,
+        )
+        copy.start()
+        flights[part] = copy
+
+    def take(part, stage):
+        _, _, _, size, offset = plans[part][stage]
+        flights[part].wait()
+        source = in_ref if stage == 0 else partial
+        rows = pl.ds(starts[part][-1], size)
+        target = out_ref if stage == count - 1 else partial
+        target[part, :, rows, :] = (
+            source[part, :, rows, :] + landed[part, :, pl.ds(offset, size), :]
+        )
+
+    def spread(part, stage):
+        axis, bit, halved, size, _ = plans[part][stage]
+        flights[part] = None
+        if not halved:
+            return
+        rows = pl.ds(starts[part][stage + 1], size)
+        copy = pltpu.make_async_remote_copy(
+            src_ref=out_ref.at[part, :, rows, :],
+            dst_ref=out_ref.at[part, :, rows, :],
+            send_sem=send_ag.at[part, stage],
+            recv_sem=recv_ag.at[part, stage],
+            device_id=partner(axis, bit),
+            device_id_type=pl.DeviceIdType.MESH,
+        )
+        copy.start()
+        flights[part] = copy
+
+    for part in range(2):
+        send(part, 0)
+    for stage in range(count):
+        for part in range(2):
+            take(part, stage)
+            if stage + 1 < count:
+                send(part, stage + 1)
+            else:
+                spread(part, stage)
+    for stage in range(count - 2, -2, -1):
+        for part in range(2):
+            if flights[part] is not None:
+                flights[part].wait()
+            if stage >= 0:
+                spread(part, stage)
+
+
+def total_over_mesh(values):
+    sizes = [(axis, lax.axis_size(axis)) for axis in ("row", "col")]
+    parts, planes, rows, lanes = values.shape
+    plans, landing = plan(sizes, rows)
+    count = len(plans[0])
+    dma = pltpu.SemaphoreType.DMA((parts, count))
+    return pl.pallas_call(
+        functools.partial(total_kernel, plans),
+        out_shape=jax.ShapeDtypeStruct(values.shape, values.dtype),
+        in_specs=[pl.BlockSpec(memory_space=pltpu.VMEM)],
+        out_specs=pl.BlockSpec(memory_space=pltpu.VMEM),
+        scratch_shapes=[
+            pltpu.VMEM(values.shape, values.dtype),
+            pltpu.VMEM((parts, planes, landing, lanes), values.dtype),
+            dma, dma, dma, dma,
+        ],
+        compiler_params=pltpu.CompilerParams(
+            collective_id=0, has_side_effects=True, vmem_limit_bytes=24 * 1024 * 1024
+        ),
+        name="total",
+    )(values)
 
 
 def shards(object_amplitude, object_phase, probe, amplitudes, positions):
@@ -189,7 +322,7 @@
     )
     extended = extended_2(object_field, (("row", 1), ("col", 2)), H)
     extended = jnp.pad(extended, ((0, 0), (0, 8), (0, 0)))
-    canvas, probe_sum, weight = frame_terms(positions, extended, probe, amplitudes)
+    canvas, sums = frame_terms(positions, extended, probe, amplitudes)
     canvas = canvas[:, : tile_side + 2 * H]
     row_edges = jnp.concatenate([canvas[:, :H], canvas[:, tile_side + H :]], axis=1)
     from_rows = extended_2(row_edges, (("row", 1),), H)
@@ -203,7 +336,10 @@
     inner = inner.at[:, :, tile_side - H :].add(from_cols[:, :, 3 * H :])
     step_size = 1.0 / (jnp.max(jnp.sum(probe * probe, axis=(0, 1))) + 1e-06)
     new_object = object_field + inner * step_size
-    total_sum, total_weight = lax.psum((probe_sum, weight), ("row", "col"))
+    total = total_over_mesh(sums)
+    total = jnp.concatenate([total[0], total[1]], axis=-1)
+    total_weight = total[-1]
+    total_sum = total[:-1].reshape(probe.shape)
     new_probe = probe + (total_sum - probe * total_weight) / (total_weight + 1e-05)
     return (new_object, new_probe)
 

time: 228 us -> 145 us (0.64)
  waiting for transfers between devices: 132 us -> 21.1 us
  Pallas kernels: 37.4 us -> 86.8 us
  between operations: 14.9 us -> 1.55 us
  other arithmetic: 13.6 us -> 9.36 us
  starting transfers between devices: 23.6 us -> 20.7 us
    psum x1 -> x0, waiting for transfers between devices: 112 us -> none  [shards(): total_sum, total_weight = lax.psum((probe_sum, weight), ('row', 'col'))]
    pallas_call x0 -> x1, Pallas kernels: none -> 47.2 us  [total_over_mesh(): pl.pallas_call(functools.partial(total_kernel, plans), out_shape=jax.Shap...]
    ppermute x4, starting transfers between devices: 17.1 us -> 14.3 us  [extended_2(): lax.ppermute(lax.slice_in_dim(block, block.shape[dim] - width, None, axis...]
  transfers between devices with their start and end apart: 9 -> 8, of which waited for: 8 -> 6; matrix products, arithmetic and copies ran while one was open for 4% -> 5% of each run, Pallas kernels for 0% -> 0%
where the time goes in v2:
time: 145 us; the launch traced here: 144 us
  Pallas kernels  86.8 us (60%)
  waiting for transfers between devices  21.1 us (15%)
  starting transfers between devices  20.7 us (14%)
  other arithmetic  9.36 us (6%)
  local copies, waits for them, and re-layouts  4.86 us (3%)
  between operations  1.55 us (1%)
    pallas_call x1, Pallas kernels, total_over_mesh(): pl.pallas_call(functools.partial(total_kernel, plans), out_shape=jax.Shap...  47.2 us
    pallas_call x1, Pallas kernels, frame_terms(): pl.pallas_call(frames_kernel, grid_spec=pltpu.PrefetchScalarGridSpec(num_...  39.6 us
    ppermute x4, waiting for transfers between devices, extended_2(): lax.ppermute(lax.slice_in_dim(block, 0, width, axis=dim), axis, backward)  16.8 us
    ppermute x4, starting transfers between devices, extended_2(): lax.ppermute(lax.slice_in_dim(block, block.shape[dim] - width, None, axis...  14.3 us
    ppermute x4, starting transfers between devices, extended_2(): lax.ppermute(lax.slice_in_dim(block, 0, width, axis=dim), axis, backward)  6.43 us
    ppermute x4, waiting for transfers between devices, extended_2(): lax.ppermute(lax.slice_in_dim(block, block.shape[dim] - width, None, axis...  4.23 us
  transfers between devices with their start and end apart: 8, of which 6 were waited for; matrix products, arithmetic and copies ran while one was open for 5% of the time, Pallas kernels for 0%

profile of v2, /device:TPU:1, one launch (start us, length us, event | category | flops | bytes accessed | tf_op | source)
XLA Modules:
  0.0 144.4 jit_solution(10283793119928722451)
XLA Ops:
  0.6 1.9 %multiply_bitcast_fusion.1 = (f32[1,256,256]{2,1,0:T(8,128)S(1)}, f32[1,256,256]{2,1,0:T(8,128)S(1)}) fusion(f32[256,256]{1,0:T(8,128)} %param.13, f32[256,256]{1,0:T(8,128)} %param.14), kind=kLoop, calls=%fused_computation.52 | loop fusion | flops 131072 | bytes 1048576 | tf_op jit(solution)/shard_map/stack | solution.py:320
  2.6 4.0 %collective-permute-start = (f32[2,64,256]{2,1,0:T(8,128)S(1)}, f32[2,64,256]{2,1,0:T(8,128)S(1)}, u32[]{:S(2)}, u32[]{:S(2)}) collective-permute-start(f32[2,64,256]{2,1,0:T(8,128)S(1)} %get-tuple-element.66), channel_id=1, source_target_pairs={{0,8},{8,16},{16,24},{1,9},{9,17},{17,25},{2,10},{10,18},{18,26},{... | collective-permute-start | bytes 393224 | tf_op jit(solution)/shard_map/ppermute | solution.py:19
  6.6 1.3 collective-permute-start.1
  7.9 1.0 fusion.24
  9.0 1.0 multiply_convert_fusion
  10.0 2.4 %collective-permute-done.1 = f32[2,64,256]{2,1,0:T(8,128)S(1)} collective-permute-done((f32[2,64,256]{2,1,0:T(8,128)S(1)}, f32[2,64,256]{2,1,0:T(8,128)S(1)}, u32[]{:S(2)}, u32[]{:S(2)}) %collective-permute-start.1) | collective-permute-done | bytes 131104 | tf_op jit(solution)/shard_map/ppermute | solution.py:22
  12.6 5.1 %collective-permute-start.2 = (f32[2,384,64]{2,1,0:T(8,128)S(1)}, f32[2,384,64]{2,1,0:T(8,128)S(1)}, u32[]{:S(2)}, u32[]{:S(2)}) collective-permute-start(f32[2,384,64]{2,1,0:T(8,128)S(1)} %get-tuple-element.64), channel_id=1, source_target_pairs={{0,1},{1,2},{2,3},{3,4},{4,5},{5,6},{6,7},{8,9},{9,10},{10,11},{11... | collective-permute-start | bytes 589832 | tf_op jit(solution)/shard_map/ppermute | solution.py:19
  17.7 1.9 %collective-permute-start.3 = (f32[2,384,64]{2,1,0:T(8,128)S(1)}, f32[2,384,64]{2,1,0:T(8,128)S(1)}, u32[]{:S(2)}, u32[]{:S(2)}) collective-permute-start(f32[2,384,64]{2,1,0:T(8,128)S(1)} %get-tuple-element.65), channel_id=1, source_target_pairs={{1,0},{2,1},{3,2},{4,3},{5,4},{6,5},{7,6},{9,8},{10,9},{11,10},{12... | collective-permute-start | bytes 589832 | tf_op jit(solution)/shard_map/ppermute | solution.py:22
  19.6 1.0 multiply_convert_fusion.2
  20.9 1.5 %collective-permute-done.2 = f32[2,384,64]{2,1,0:T(8,128)S(1)} collective-permute-done((f32[2,384,64]{2,1,0:T(8,128)S(1)}, f32[2,384,64]{2,1,0:T(8,128)S(1)}, u32[]{:S(2)}, u32[]{:S(2)}) %collective-permute-start.2) | collective-permute-done | bytes 196640 | tf_op jit(solution)/shard_map/ppermute | solution.py:19
  22.4 5.9 %collective-permute-done.3 = f32[2,384,64]{2,1,0:T(8,128)S(1)} collective-permute-done((f32[2,384,64]{2,1,0:T(8,128)S(1)}, f32[2,384,64]{2,1,0:T(8,128)S(1)}, u32[]{:S(2)}, u32[]{:S(2)}) %collective-permute-start.3) | collective-permute-done | bytes 196640 | tf_op jit(solution)/shard_map/ppermute | solution.py:22
  28.7 39.6 %frames.1 = (f32[2,392,384]{2,1,0:T(8,128)S(1)}, f32[2,9,256,128]{3,2,1,0:T(8,128)}) custom-call(s32[8,2]{1,0:T(8,128)S(1)} %copy.8.pos_ref, f32[2,392,384]{2,1,0:T(8,128)S(1)} %select_maximum_fusion.ext_ref, f32[4,2,256,256]{3,2,1,0:T(8,128)} %probe_ref.1, f32[8,256,256]{2,1,0:T(8,128)} %amp_ref.1, bf16[512,512]{1,0:T(8,128)(2,1)S(1)} %get-tuple-element.74.fl_ref, ...), custom_call_target="tpu_custom_call" | custom-call | tf_op jit(solution)/shard_map/frames/pallas_call | solution.py:161
  68.3 1.7 %copy-done = f32[2,9,256,128]{3,2,1,0:T(8,128)S(1)} copy-done((f32[2,9,256,128]{3,2,1,0:T(8,128)S(1)}, f32[2,9,256,128]{3,2,1,0:T(8,128)}, u32[]{:S(2)}) %copy-start) | copy-done | bytes 2359320
  70.0 47.2 %total.1 = f32[2,9,256,128]{3,2,1,0:T(8,128)S(1)} custom-call(f32[2,9,256,128]{3,2,1,0:T(8,128)S(1)} %copy-done), custom_call_target="tpu_custom_call" | custom-call | tf_op jit(solution)/shard_map/total/pallas_call | solution.py:301
  117.3 1.3 collective-permute-start.4
  118.9 1.3 collective-permute-start.5
  120.2 2.7 %collective-permute-done.4 = f32[2,64,384]{2,1,0:T(8,128)S(1)} collective-permute-done((f32[2,64,384]{2,1,0:T(8,128)S(1)}, f32[2,64,384]{2,1,0:T(8,128)S(1)}, u32[]{:S(2)}, u32[]{:S(2)}) %collective-permute-start.4) | collective-permute-done | bytes 196640 | tf_op jit(solution)/shard_map/ppermute | solution.py:19
  123.0 4.1 %collective-permute-done.5 = f32[2,64,384]{2,1,0:T(8,128)S(1)} collective-permute-done((f32[2,64,384]{2,1,0:T(8,128)S(1)}, f32[2,64,384]{2,1,0:T(8,128)S(1)}, u32[]{:S(2)}, u32[]{:S(2)}) %collective-permute-start.5) | collective-permute-done | bytes 196640 | tf_op jit(solution)/shard_map/ppermute | solution.py:22
  127.2 3.9 %collective-permute-start.6 = (f32[2,256,64]{2,1,0:T(8,128)S(1)}, f32[2,256,64]{2,1,0:T(8,128)S(1)}, u32[]{:S(2)}, u32[]{:S(2)}) collective-permute-start(f32[2,256,64]{2,1,0:T(8,128)S(1)} %get-tuple-element.63), channel_id=1, source_target_pairs={{0,1},{1,2},{2,3},{3,4},{4,5},{5,6},{6,7},{8,9},{9,10},{10,11},{11... | collective-permute-start | bytes 393224 | tf_op jit(solution)/shard_map/ppermute | solution.py:19
  131.1 1.8 %divide_add_fusion = (f32[4,2,256,256]{3,2,1,0:T(8,128)}, f32[256,256]{1,0:T(8,128)S(1)}) fusion(f32[4,2,256,256]{3,2,1,0:T(8,128)S(1)} %copy-done.1, f32[256,256]{1,0:T(8,128)S(1)} %get-tuple-element.54, f32[256,256]{1,0:T(8,128)S(1)} %get-tuple-element.55, f32[9,256,128]{2,1,0:T(8,128)S(1)} %get-tuple-element.56, f32[9,256,128]{2,1,0:T(8,128)S(1)} %get-tuple-element.57), kind=kLoop, calls=%fused_computation.3 | loop fusion | flops 3604480 | bytes 7340032 | tf_op jit(solution)/shard_map/add | solution.py:343
  134.5 1.9 %collective-permute-start.7 = (f32[2,256,64]{2,1,0:T(8,128)S(1)}, f32[2,256,64]{2,1,0:T(8,128)S(1)}, u32[]{:S(2)}, u32[]{:S(2)}) collective-permute-start(f32[2,256,64]{2,1,0:T(8,128)S(1)} %get-tuple-element.62), channel_id=1, source_target_pairs={{1,0},{2,1},{3,2},{4,3},{5,4},{6,5},{7,6},{9,8},{10,9},{11,10},{12... | collective-permute-start | bytes 393224 | tf_op jit(solution)/shard_map/ppermute | solution.py:22
  136.6 1.1 scatter-add.16
  137.7 4.5 %collective-permute-done.7 = f32[2,256,64]{2,1,0:T(8,128)S(1)} collective-permute-done((f32[2,256,64]{2,1,0:T(8,128)S(1)}, f32[2,256,64]{2,1,0:T(8,128)S(1)}, u32[]{:S(2)}, u32[]{:S(2)}) %collective-permute-start.7) | collective-permute-done | bytes 131104 | tf_op jit(solution)/shard_map/ppermute | solution.py:22
  142.3 1.2 scatter-add.19
  (25 shorter events, 3.5 us)
Async XLA Ops:
  2.6 7.4 %collective-permute-start = (f32[2,64,256]{2,1,0:T(8,128)S(1)}, f32[2,64,256]{2,1,0:T(8,128)S(1)}, u32[]{:S(2)}, u32[]{:S(2)}) collective-permute-start(f32[2,64,256]{2,1,0:T(8,128)S(1)} %get-tuple-element.66), channel_id=1, source_target_pairs={{0,8},{8,16},{16,24},{1,9},{9,17},{17,25},{2,10},{10,18},{18,26},{... | collective-permute-start | bytes 393224 | tf_op jit(solution)/shard_map/ppermute | solution.py:19
  6.6 5.7 %collective-permute-start.1 = (f32[2,64,256]{2,1,0:T(8,128)S(1)}, f32[2,64,256]{2,1,0:T(8,128)S(1)}, u32[]{:S(2)}, u32[]{:S(2)}) collective-permute-start(f32[2,64,256]{2,1,0:T(8,128)S(1)} %get-tuple-element.67), channel_id=1, source_target_pairs={{8,0},{16,8},{24,16},{9,1},{17,9},{25,17},{10,2},{18,10},{26,18},{... | collective-permute-start | bytes 393224 | tf_op jit(solution)/shard_map/ppermute | solution.py:22
  12.4 8.2 %copy-start.2 = (s32[8,2]{0,1:T(2,128)S(1)}, s32[8,2]{0,1:T(2,128)}, u32[]{:S(2)}) copy-start(s32[8,2]{0,1:T(2,128)} %param.17) | copy-start | bytes 196
  12.6 9.8 %collective-permute-start.2 = (f32[2,384,64]{2,1,0:T(8,128)S(1)}, f32[2,384,64]{2,1,0:T(8,128)S(1)}, u32[]{:S(2)}, u32[]{:S(2)}) collective-permute-start(f32[2,384,64]{2,1,0:T(8,128)S(1)} %get-tuple-element.64), channel_id=1, source_target_pairs={{0,1},{1,2},{2,3},{3,4},{4,5},{5,6},{6,7},{8,9},{9,10},{10,11},{11... | collective-permute-start | bytes 589832 | tf_op jit(solution)/shard_map/ppermute | solution.py:19
  17.7 10.6 %collective-permute-start.3 = (f32[2,384,64]{2,1,0:T(8,128)S(1)}, f32[2,384,64]{2,1,0:T(8,128)S(1)}, u32[]{:S(2)}, u32[]{:S(2)}) collective-permute-start(f32[2,384,64]{2,1,0:T(8,128)S(1)} %get-tuple-element.65), channel_id=1, source_target_pairs={{1,0},{2,1},{3,2},{4,3},{5,4},{6,5},{7,6},{9,8},{10,9},{11,10},{12... | collective-permute-start | bytes 589832 | tf_op jit(solution)/shard_map/ppermute | solution.py:22
  68.3 1.7 %copy-start = (f32[2,9,256,128]{3,2,1,0:T(8,128)S(1)}, f32[2,9,256,128]{3,2,1,0:T(8,128)}, u32[]{:S(2)}) copy-start(f32[2,9,256,128]{3,2,1,0:T(8,128)} %get-tuple-element.53.in_ref) | copy-start | bytes 7077892
  117.3 5.7 %collective-permute-start.4 = (f32[2,64,384]{2,1,0:T(8,128)S(1)}, f32[2,64,384]{2,1,0:T(8,128)S(1)}, u32[]{:S(2)}, u32[]{:S(2)}) collective-permute-start(f32[2,64,384]{2,1,0:T(8,128)S(1)} %get-tuple-element.61), channel_id=1, source_target_pairs={{0,8},{8,16},{16,24},{1,9},{9,17},{17,25},{2,10},{10,18},{18,26},{... | collective-permute-start | bytes 589832 | tf_op jit(solution)/shard_map/ppermute | solution.py:19
  118.9 8.2 %collective-permute-start.5 = (f32[2,64,384]{2,1,0:T(8,128)S(1)}, f32[2,64,384]{2,1,0:T(8,128)S(1)}, u32[]{:S(2)}, u32[]{:S(2)}) collective-permute-start(f32[2,64,384]{2,1,0:T(8,128)S(1)} %get-tuple-element.60), channel_id=1, source_target_pairs={{8,0},{16,8},{24,16},{9,1},{17,9},{25,17},{10,2},{18,10},{26,18},{... | collective-permute-start | bytes 589832 | tf_op jit(solution)/shard_map/ppermute | solution.py:22
  120.2 10.9 %copy-start.1 = (f32[4,2,256,256]{3,2,1,0:T(8,128)S(1)}, f32[4,2,256,256]{3,2,1,0:T(8,128)}, u32[]{:S(2)}) copy-start(f32[4,2,256,256]{3,2,1,0:T(8,128)} %probe_ref.1) | copy-start | bytes 6291460
  127.2 9.2 %collective-permute-start.6 = (f32[2,256,64]{2,1,0:T(8,128)S(1)}, f32[2,256,64]{2,1,0:T(8,128)S(1)}, u32[]{:S(2)}, u32[]{:S(2)}) collective-permute-start(f32[2,256,64]{2,1,0:T(8,128)S(1)} %get-tuple-element.63), channel_id=1, source_target_pairs={{0,1},{1,2},{2,3},{3,4},{4,5},{5,6},{6,7},{8,9},{9,10},{10,11},{11... | collective-permute-start | bytes 393224 | tf_op jit(solution)/shard_map/ppermute | solution.py:19
  134.5 7.7 %collective-permute-start.7 = (f32[2,256,64]{2,1,0:T(8,128)S(1)}, f32[2,256,64]{2,1,0:T(8,128)S(1)}, u32[]{:S(2)}, u32[]{:S(2)}) collective-permute-start(f32[2,256,64]{2,1,0:T(8,128)S(1)} %get-tuple-element.62), channel_id=1, source_target_pairs={{1,0},{2,1},{3,2},{4,3},{5,4},{6,5},{7,6},{9,8},{10,9},{11,10},{12... | collective-permute-start | bytes 393224 | tf_op jit(solution)/shard_map/ppermute | solution.py:22

commit v3 on v2

--- a/solution.py
+++ b/solution.py
@@ -11,17 +11,127 @@
 H = 64
 
 
-def extended_2(block, sides, width):
-    for axis, dim in sides:
-        count = lax.axis_size(axis)
-        forward = [(i, i + 1) for i in range(count - 1)]
-        backward = [(target, source) for source, target in forward]
-        low = lax.ppermute(
-            lax.slice_in_dim(block, block.shape[dim] - width, None, axis=dim), axis, forward
+def here():
+    return {"row": lax.axis_index("row"), "col": lax.axis_index("col")}
+
+
+def sides_of(axis, coords):
+    count = lax.axis_size(axis)
+    found = []
+    for move in (-1, 1):
+        other = dict(coords)
+        other[axis] = lax.rem(coords[axis] + move + count, count)
+        inside = coords[axis] > 0 if move < 0 else coords[axis] < count - 1
+        found.append(((other["row"], other["col"]), inside))
+    return found
+
+
+def greet(devices):
+    barrier = pltpu.get_barrier_semaphore()
+    for device in devices:
+        pl.semaphore_signal(barrier, inc=1, device_id=device, device_id_type=pl.DeviceIdType.MESH)
+    pl.semaphore_wait(barrier, len(devices))
+
+
+def swap_starts(axis, coords, copies):
+    for (device, inside), copy in zip(sides_of(axis, coords), copies):
+
+        @pl.when(inside)
+        def _(copy=copy):
+            copy.start()
+
+
+def swap_waits(axis, coords, copies):
+    for (device, inside), copy, back in zip(sides_of(axis, coords), copies, copies[::-1]):
+
+        @pl.when(inside)
+        def _(copy=copy, back=back):
+            copy.wait_send()
+            back.wait_recv()
+
+
+def remote(source, target, send, recv, device):
+    return pltpu.make_async_remote_copy(
+        src_ref=source, dst_ref=target, send_sem=send, recv_sem=recv,
+        device_id=device, device_id_type=pl.DeviceIdType.MESH,
+    )
+
+
+def edge_mask(shape):
+    return lax.broadcasted_iota(jnp.int32, shape, 1) < H
+
+
+def extend_kernel(tile_ref, ext_ref, edge, mid, from_cols, from_rows, send, recv):
+    coords = here()
+    side = tile_ref.shape[1]
+    row_sides, col_sides = sides_of("row", coords), sides_of("col", coords)
+    greet([device for device, _ in row_sides + col_sides])
+    for c in range(2):
+        edge[c] = pltpu.roll(tile_ref[c], H, axis=1)[:, : 2 * H]
+    copies = [
+        remote(edge, from_cols.at[1 - k], send.at[0, k], recv.at[0, k], col_sides[k][0])
+        for k in range(2)
+    ]
+    swap_starts("col", coords, copies)
+    swap_waits("col", coords, copies)
+    step = 64
+    has_low, has_high = col_sides[0][1], col_sides[1][1]
+    for c in range(2):
+        for r in range(0, side, step):
+            rows = pl.ds(r, step)
+            first = edge_mask((step, 2 * H))
+            zero = jnp.zeros((step, 2 * H), jnp.float32)
+            low = jnp.where(jnp.logical_and(first, has_low), from_cols[0, c, rows, :], zero)
+            high = jnp.where(
+                jnp.logical_and(jnp.logical_not(first), has_high), from_cols[1, c, rows, :], zero
+            )
+            rest = pltpu.roll(low + high, H, axis=1)
+            line = pltpu.roll(jnp.concatenate([tile_ref[c, rows, :], rest], axis=1), H, axis=1)
+            mid[c, rows, :] = line
+            ext_ref[c, pl.ds(H + r, step), :] = line
+    tops = [pl.ds(0, H), pl.ds(side - H, H)]
+    copies = [
+        remote(
+            mid.at[:, tops[k], :], from_rows.at[1 - k], send.at[1, k], recv.at[1, k],
+            row_sides[k][0],
         )
-        high = lax.ppermute(lax.slice_in_dim(block, 0, width, axis=dim), axis, backward)
-        block = jnp.concatenate([low, block, high], axis=dim)
-    return block
+        for k in range(2)
+    ]
+    swap_starts("row", coords, copies)
+    swap_waits("row", coords, copies)
+    places = [0, side + H]
+    for k in range(2):
+        for c in range(2):
+            got = from_rows[k, c]
+            ext_ref[c, pl.ds(places[k], H), :] = jnp.where(
+                row_sides[k][1], got, jnp.zeros_like(got)
+            )
+    for c in range(2):
+        ext_ref[c, pl.ds(side + 2 * H, 8), :] = jnp.zeros((8, side + 2 * H), jnp.float32)
+
+
+def extend(tile):
+    side = tile.shape[1]
+    wide = side + 2 * H
+    f32 = jnp.float32
+    dma = pltpu.SemaphoreType.DMA((2, 2))
+    return pl.pallas_call(
+        extend_kernel,
+        out_shape=jax.ShapeDtypeStruct((2, wide + 8, wide), f32),
+        in_specs=[pl.BlockSpec(memory_space=pltpu.VMEM)],
+        out_specs=pl.BlockSpec(memory_space=pltpu.VMEM),
+        scratch_shapes=[
+            pltpu.VMEM((2, side, 2 * H), f32),
+            pltpu.VMEM((2, side, wide), f32),
+            pltpu.VMEM((2, 2, side, 2 * H), f32),
+            pltpu.VMEM((2, 2, H, wide), f32),
+            dma, dma,
+        ],
+        compiler_params=pltpu.CompilerParams(
+            collective_id=1, has_side_effects=True, vmem_limit_bytes=16 * 1024 * 1024
+        ),
+        name="extend",
+    )(tile)
 
 
 def fourier_tables(side, sign):
@@ -207,8 +317,11 @@
     return plans, max(stages[-1][3] + stages[-1][4] for stages in plans)
 
 
-def total_kernel(plans, in_ref, out_ref, partial, landed, send_rs, recv_rs, send_ag, recv_ag):
-    coords = {"row": lax.axis_index("row"), "col": lax.axis_index("col")}
+def total_kernel(
+    plans, in_ref, canvas_ref, out_ref, inner_ref, partial, landed, send_rs, recv_rs, send_ag, recv_ag,
+    mid, edge, from_cols, from_rows, send_halo, recv_halo,
+):
+    coords = here()
 
     def bit_of(axis, bit):
         return lax.rem(coords[axis] // (1 << bit), 2)
@@ -218,12 +331,57 @@
         flipped[axis] = coords[axis] + (1 - 2 * bit_of(axis, bit)) * (1 << bit)
         return (flipped["row"], flipped["col"])
 
-    barrier = pltpu.get_barrier_semaphore()
-    for axis, bit, *_ in plans[0]:
-        pl.semaphore_signal(
-            barrier, inc=1, device_id=partner(axis, bit), device_id_type=pl.DeviceIdType.MESH
+    row_sides, col_sides = sides_of("row", coords), sides_of("col", coords)
+    greet(
+        [partner(axis, bit) for axis, bit, *_ in plans[0]]
+        + [device for device, _ in row_sides + col_sides]
+    )
+    side = inner_ref.shape[1]
+    places = [0, side + H]
+    row_copies = [
+        remote(
+            canvas_ref.at[:, pl.ds(places[k], H), :], from_rows.at[1 - k],
+            send_halo.at[0, k], recv_halo.at[0, k], row_sides[k][0],
         )
-    pl.semaphore_wait(barrier, len(plans[0]))
+        for k in range(2)
+    ]
+    col_copies = [
+        remote(edge, from_cols.at[1 - k], send_halo.at[1, k], recv_halo.at[1, k], col_sides[k][0])
+        for k in range(2)
+    ]
+
+    def rows_done():
+        swap_waits("row", coords, row_copies)
+        for c in range(2):
+            for r in range(0, side, H):
+                part = canvas_ref[c, pl.ds(H + r, H), :]
+                for k, at in ((0, 0), (1, side - H)):
+                    if r == at:
+                        got = from_rows[k, c]
+                        part = part + jnp.where(row_sides[k][1], got, jnp.zeros_like(got))
+                mid[c, pl.ds(r, H), :] = part
+                edge[c, pl.ds(r, H), :] = pltpu.roll(part, H, axis=1)[:, : 2 * H]
+        swap_starts("col", coords, col_copies)
+
+    def cols_done():
+        swap_waits("col", coords, col_copies)
+        first = edge_mask((H, 2 * H))
+        zero = jnp.zeros((H, 2 * H), jnp.float32)
+        masks = [
+            jnp.logical_and(first, col_sides[0][1]),
+            jnp.logical_and(jnp.logical_not(first), col_sides[1][1]),
+        ]
+        for c in range(2):
+            for r in range(0, side, H):
+                rows = pl.ds(r, H)
+                part = mid[c, rows, :]
+                part = pltpu.roll(part, part.shape[1] - H, axis=1)[:, :side]
+                pieces = []
+                for k in range(2):
+                    pieces.append(jnp.where(masks[k], from_cols[k, c, rows, :], zero))
+                if side > 4 * H:
+                    pieces.insert(1, jnp.zeros((H, side - 4 * H), jnp.float32))
+                inner_ref[c, rows, :] = part + jnp.concatenate(pieces, axis=1)
 
     count = len(plans[0])
     starts = [[0], [0]]
@@ -277,7 +435,10 @@
 
     for part in range(2):
         send(part, 0)
+    swap_starts("row", coords, row_copies)
     for stage in range(count):
+        if stage == 1:
+            rows_done()
         for part in range(2):
             take(part, stage)
             if stage + 1 < count:
@@ -290,53 +451,52 @@
                 flights[part].wait()
             if stage >= 0:
                 spread(part, stage)
-
-
-def total_over_mesh(values):
+        if stage == 0:
+            cols_done()
+
+
+def total_over_mesh(values, canvas):
     sizes = [(axis, lax.axis_size(axis)) for axis in ("row", "col")]
     parts, planes, rows, lanes = values.shape
     plans, landing = plan(sizes, rows)
+    wide = canvas.shape[2]
+    side = wide - 2 * H
     count = len(plans[0])
     dma = pltpu.SemaphoreType.DMA((parts, count))
     return pl.pallas_call(
         functools.partial(total_kernel, plans),
-        out_shape=jax.ShapeDtypeStruct(values.shape, values.dtype),
-        in_specs=[pl.BlockSpec(memory_space=pltpu.VMEM)],
-        out_specs=pl.BlockSpec(memory_space=pltpu.VMEM),
+        out_shape=[
+            jax.ShapeDtypeStruct(values.shape, values.dtype),
+            jax.ShapeDtypeStruct((2, side, side), values.dtype),
+        ],
+        in_specs=[pl.BlockSpec(memory_space=pltpu.VMEM)] * 2,
+        out_specs=[pl.BlockSpec(memory_space=pltpu.VMEM)] * 2,
         scratch_shapes=[
             pltpu.VMEM(values.shape, values.dtype),
             pltpu.VMEM((parts, planes, landing, lanes), values.dtype),
             dma, dma, dma, dma,
+            pltpu.VMEM((2, side, wide), values.dtype),
+            pltpu.VMEM((2, side, 2 * H), values.dtype),
+            pltpu.VMEM((2, 2, side, 2 * H), values.dtype),
+            pltpu.VMEM((2, 2, H, wide), values.dtype),
+            pltpu.SemaphoreType.DMA((2, 2)),
+            pltpu.SemaphoreType.DMA((2, 2)),
         ],
         compiler_params=pltpu.CompilerParams(
             collective_id=0, has_side_effects=True, vmem_limit_bytes=24 * 1024 * 1024
         ),
         name="total",
-    )(values)
+    )(values, canvas)
 
 
 def shards(object_amplitude, object_phase, probe, amplitudes, positions):
-    tile_side = object_amplitude.shape[0]
     object_field = jnp.stack(
         [object_amplitude * jnp.cos(object_phase), object_amplitude * jnp.sin(object_phase)]
     )
-    extended = extended_2(object_field, (("row", 1), ("col", 2)), H)
-    extended = jnp.pad(extended, ((0, 0), (0, 8), (0, 0)))
-    canvas, sums = frame_terms(positions, extended, probe, amplitudes)
-    canvas = canvas[:, : tile_side + 2 * H]
-    row_edges = jnp.concatenate([canvas[:, :H], canvas[:, tile_side + H :]], axis=1)
-    from_rows = extended_2(row_edges, (("row", 1),), H)
-    canvas = canvas.at[:, H : 2 * H].add(from_rows[:, :H])
-    canvas = canvas.at[:, tile_side : tile_side + H].add(from_rows[:, 3 * H :])
-    middle = canvas[:, H : tile_side + H]
-    col_edges = jnp.concatenate([middle[:, :, :H], middle[:, :, tile_side + H :]], axis=2)
-    from_cols = extended_2(col_edges, (("col", 2),), H)
-    inner = middle[:, :, H : tile_side + H]
-    inner = inner.at[:, :, :H].add(from_cols[:, :, :H])
-    inner = inner.at[:, :, tile_side - H :].add(from_cols[:, :, 3 * H :])
+    canvas, sums = frame_terms(positions, extend(object_field), probe, amplitudes)
+    total, inner = total_over_mesh(sums, canvas)
     step_size = 1.0 / (jnp.max(jnp.sum(probe * probe, axis=(0, 1))) + 1e-06)
     new_object = object_field + inner * step_size
-    total = total_over_mesh(sums)
     total = jnp.concatenate([total[0], total[1]], axis=-1)
     total_weight = total[-1]
     total_sum = total[:-1].reshape(probe.shape)

time: 145 us -> 121 us (0.83)
  waiting for transfers between devices: 21.1 us -> 0 us
  starting transfers between devices: 20.7 us -> 0 us
  Pallas kernels: 86.8 us -> 106 us
    ppermute x8 -> x0, waiting for transfers between devices: 21.1 us -> none  [the longest x4 16.8 us: extended_2(): lax.ppermute(lax.slice_in_dim(block, 0, width, axis=dim), axis, backward)]
    ppermute x8 -> x0, starting transfers between devices: 20.7 us -> none  [the longest x4 14.3 us: extended_2(): lax.ppermute(lax.slice_in_dim(block, block.shape[dim] - width, None, axis...]
    pallas_call x1 -> x2, Pallas kernels: 47.2 us -> 66.6 us  [the longest x1 50.8 us: total_over_mesh(): pl.pallas_call(functools.partial(total_kernel, plans), out_shape=[jax.Sha...]
    scatter-add x2 -> x0, local copies, waits for them, and re-layouts: 2.3 us -> none  [the longest x1 1.19 us: shards(): inner = inner.at[:, :, tile_side - H:].add(from_cols[:, :, 3 * H:])]
    unnamed x7 -> x5, local copies, waits for them, and re-layouts: 1.76 us -> 3.96 us
  transfers between devices with their start and end apart: 8 -> 0, of which waited for: 6 -> 0; matrix products, arithmetic and copies ran while one was open for 5% -> 0% of each run, Pallas kernels for 0% -> 0%
where the time goes in v3:
time: 121 us; the launch traced here: 120 us
  Pallas kernels  106 us (88%)
  other arithmetic  8.48 us (7%)
  local copies, waits for them, and re-layouts  4.12 us (3%)
  between operations  1.4 us (1%)
    pallas_call x1, Pallas kernels, total_over_mesh(): pl.pallas_call(functools.partial(total_kernel, plans), out_shape=[jax.Sha...  50.8 us
    pallas_call x1, Pallas kernels, frame_terms(): pl.pallas_call(frames_kernel, grid_spec=pltpu.PrefetchScalarGridSpec(num_...  39.6 us
    pallas_call x1, Pallas kernels, extend(): pl.pallas_call(extend_kernel, out_shape=jax.ShapeDtypeStruct((2, wide + 8...  15.8 us
    unnamed x5, local copies, waits for them, and re-layouts  3.96 us

profile of v3, /device:TPU:1, one launch (start us, length us, event | category | flops | bytes accessed | tf_op | source)
XLA Modules:
  0.0 120.2 jit_solution(3360067560262926179)
XLA Ops:
  0.6 0.8 copy.8.pos_ref
  1.4 1.0 multiply_convert_fusion.2
  2.4 1.0 fusion.13
  3.4 1.0 multiply_convert_fusion
  4.4 1.9 %multiply_bitcast_fusion.1 = (f32[1,256,256]{2,1,0:T(8,128)S(1)}, f32[1,256,256]{2,1,0:T(8,128)S(1)}) fusion(f32[256,256]{1,0:T(8,128)} %param.5, f32[256,256]{1,0:T(8,128)} %param.6), kind=kLoop, calls=%fused_computation.35 | loop fusion | flops 131072 | bytes 1048576 | tf_op jit(solution)/shard_map/stack | solution.py:493
  6.4 15.8 %extend.1.ext_ref = f32[2,392,384]{2,1,0:T(8,128)S(1)} custom-call(f32[2,256,256]{2,1,0:T(8,128)S(1)} %pad_maximum_fusion.8.tile_ref), custom_call_target="tpu_custom_call" | custom-call | tf_op jit(solution)/shard_map/extend/pallas_call | solution.py:118
  22.2 0.2 fusion.4
  22.3 39.6 %frames.1 = (f32[2,392,384]{2,1,0:T(8,128)S(1)}, f32[2,9,256,128]{3,2,1,0:T(8,128)}) custom-call(s32[8,2]{1,0:T(8,128)S(1)} %copy.8.pos_ref, f32[2,392,384]{2,1,0:T(8,128)S(1)} %extend.1.ext_ref, f32[4,2,256,256]{3,2,1,0:T(8,128)} %probe_ref.1, f32[8,256,256]{2,1,0:T(8,128)} %amp_ref.1, bf16[512,512]{1,0:T(8,128)(2,1)S(1)} %get-tuple-element.22.fl_ref, ...), custom_call_target="tpu_custom_call" | custom-call | tf_op jit(solution)/shard_map/frames/pallas_call | solution.py:271
  61.9 0.0 copy-start
  61.9 1.7 %copy-done = f32[2,9,256,128]{3,2,1,0:T(8,128)S(1)} copy-done((f32[2,9,256,128]{3,2,1,0:T(8,128)S(1)}, f32[2,9,256,128]{3,2,1,0:T(8,128)}, u32[]{:S(2)}) %copy-start) | copy-done | bytes 2359320
  63.6 50.8 %total.1 = (f32[2,9,256,128]{3,2,1,0:T(8,128)S(1)}, f32[2,256,256]{2,1,0:T(8,128)S(1)}) custom-call(f32[2,9,256,128]{3,2,1,0:T(8,128)S(1)} %copy-done, f32[2,392,384]{2,1,0:T(8,128)S(1)} %get-tuple-element.7.canvas_ref), custom_call_target="tpu_custom_call" | custom-call | tf_op jit(solution)/shard_map/total/pallas_call | solution.py:466
  114.4 0.2 slice_bitcast_fusion
  114.6 0.0 copy-start.1
  114.6 1.5 %copy-done.1 = f32[4,2,256,256]{3,2,1,0:T(8,128)S(1)} copy-done((f32[4,2,256,256]{3,2,1,0:T(8,128)S(1)}, f32[4,2,256,256]{3,2,1,0:T(8,128)}, u32[]{:S(2)}) %copy-start.1) | copy-done | bytes 2097176
  116.2 1.8 %divide_add_fusion = (f32[4,2,256,256]{3,2,1,0:T(8,128)}, f32[256,256]{1,0:T(8,128)S(1)}) fusion(f32[4,2,256,256]{3,2,1,0:T(8,128)S(1)} %copy-done.1, f32[256,256]{1,0:T(8,128)S(1)} %get-tuple-element.10, f32[256,256]{1,0:T(8,128)S(1)} %get-tuple-element.11, f32[9,256,128]{2,1,0:T(8,128)S(1)} %get-tuple-element.12, f32[9,256,128]{2,1,0:T(8,128)S(1)} %get-tuple-element.13), kind=kLoop, calls=%fused_computation.3 | loop fusion | flops 3604480 | bytes 7340032 | tf_op jit(solution)/shard_map/add | solution.py:503
  117.9 0.7 reduce_max.9
  119.3 0.9 multiply_add_fusion
  (2 shorter events, 0.1 us)
Async XLA Ops:
  61.9 1.7 %copy-start = (f32[2,9,256,128]{3,2,1,0:T(8,128)S(1)}, f32[2,9,256,128]{3,2,1,0:T(8,128)}, u32[]{:S(2)}) copy-start(f32[2,9,256,128]{3,2,1,0:T(8,128)} %get-tuple-element.6.in_ref) | copy-start | bytes 7077892
  114.6 1.6 %copy-start.1 = (f32[4,2,256,256]{3,2,1,0:T(8,128)S(1)}, f32[4,2,256,256]{3,2,1,0:T(8,128)}, u32[]{:S(2)}) copy-start(f32[4,2,256,256]{3,2,1,0:T(8,128)} %probe_ref.1) | copy-start | bytes 6291460

commit v4 on v3

--- a/solution.py
+++ b/solution.py
@@ -3,6 +3,7 @@
 
 import jax
 import jax.numpy as jnp
+import numpy as np
 from jax import lax
 from jax.experimental import pallas as pl
 from jax.experimental.pallas import tpu as pltpu
@@ -134,20 +135,14 @@
     )(tile)
 
 
-def fourier_tables(side, sign):
-    counter = jnp.arange(side, dtype=jnp.int32)
-    product = counter[:, None] * counter[None, :] % side
-    angle = product.astype(jnp.float32) * (2.0 * math.pi / side)
-    norming = 1.0 / math.sqrt(side)
-    real = (jnp.cos(angle) * norming).astype(jnp.bfloat16)
-    imag = (sign * jnp.sin(angle) * norming).astype(jnp.bfloat16)
-    left = jnp.concatenate(
-        [jnp.concatenate([real, -imag], axis=1), jnp.concatenate([imag, real], axis=1)], axis=0
-    )
-    right = jnp.concatenate(
-        [jnp.concatenate([real, imag], axis=1), jnp.concatenate([-imag, real], axis=1)], axis=0
-    )
-    return left, right
+def fourier_tables(side):
+    counter = np.arange(side, dtype=np.int64)
+    angle = (counter[:, None] * counter[None, :] % side) * (2.0 * math.pi / side)
+    real = np.cos(angle) / math.sqrt(side)
+    imag = -np.sin(angle) / math.sqrt(side)
+    left = np.block([[real, -imag], [imag, real]])
+    right = np.block([[real, imag], [-imag, real]])
+    return [table.astype(np.float32).astype(jnp.bfloat16) for table in (left, right)]
 
 
 def dot(a, b):
@@ -155,8 +150,8 @@
 
 
 def frames_kernel(
-    pos_ref, ext_ref, probe_ref, amp_ref, fl_ref, fr_ref, il_ref, ir_ref,
-    canvas_ref, s_ref,
+    pos_ref, ext_ref, probe_ref, amp_ref, left_ref, right_ref,
+    canvas_ref, s_ref, step_ref,
     o_scr, x_scr, h_scr, spec_scr, int_scr, p2_scr, g_scr,
 ):
     frame = pl.program_id(0)
@@ -183,6 +178,8 @@
                 for c in range(2):
                     total += probe_ref[m, c, rows, :] * probe_ref[m, c, rows, :]
             p2_scr[rows, :] = total
+        peak = jnp.max(jnp.max(p2_scr[...], axis=0, keepdims=True), axis=1, keepdims=True)
+        step_ref[...] = jnp.broadcast_to(1.0 / (peak + 1e-06), step_ref.shape)
 
     r0 = pos_ref[frame, 0] + H
     c0 = pos_ref[frame, 1] + H
@@ -206,10 +203,10 @@
             o_r, o_i = o_scr[0, rows, :], o_scr[1, rows, :]
             x_scr[m, rows, :] = (pr * o_r - pi * o_i).astype(jnp.bfloat16)
             x_scr[m, under, :] = (pr * o_i + pi * o_r).astype(jnp.bfloat16)
-        half = dot(fl_ref[...], x_scr[m]).astype(jnp.bfloat16)
+        half = dot(left_ref[...], x_scr[m]).astype(jnp.bfloat16)
         h_scr[m, :, :n] = half[:n]
         h_scr[m, :, n:] = half[n:]
-        spec_scr[m] = dot(h_scr[m], fr_ref[...])
+        spec_scr[m] = dot(h_scr[m], right_ref[...])
 
     for rows in chunks:
         total = jnp.zeros((step, n), jnp.float32)
@@ -223,10 +220,10 @@
             fac = int_scr[rows, :]
             x_scr[m, rows, :] = (spec_scr[m, rows, :n] * fac).astype(jnp.bfloat16)
             x_scr[m, under, :] = (spec_scr[m, rows, n:] * fac).astype(jnp.bfloat16)
-        half = dot(il_ref[...], x_scr[m]).astype(jnp.bfloat16)
+        half = dot(right_ref[...], x_scr[m]).astype(jnp.bfloat16)
         h_scr[m, :, :n] = half[:n]
         h_scr[m, :, n:] = half[n:]
-        spec_scr[m] = dot(h_scr[m], ir_ref[...])
+        spec_scr[m] = dot(h_scr[m], left_ref[...])
         for rows in chunks:
             br, bi = spec_scr[m, rows, :n], spec_scr[m, rows, n:]
             o_r, o_i = o_scr[0, rows, :], o_scr[1, rows, :]
@@ -260,8 +257,7 @@
     frames = amplitudes.shape[0]
     wide = extended.shape[2]
     high = extended.shape[1]
-    forward = fourier_tables(n, -1.0)
-    inverse = fourier_tables(n, 1.0)
+    tables = [jnp.asarray(table) for table in fourier_tables(n)]
     f32 = jnp.float32
     sums = (2, 2 * modes + 1, n, n // 2)
 
@@ -278,8 +274,8 @@
                 whole(probe.shape),
                 pl.BlockSpec((1, n, n), lambda i, pos: (i, 0, 0)),
             ]
-            + [whole((2 * n, 2 * n))] * 4,
-            out_specs=[whole((2, high, wide)), whole(sums)],
+            + [whole((2 * n, 2 * n))] * 2,
+            out_specs=[whole((2, high, wide)), whole(sums), whole((8, 128))],
             scratch_shapes=[
                 pltpu.VMEM((2, n, n), f32),
                 pltpu.VMEM((modes, 2 * n, n), jnp.bfloat16),
@@ -293,10 +289,11 @@
         out_shape=[
             jax.ShapeDtypeStruct((2, high, wide), f32),
             jax.ShapeDtypeStruct(sums, f32),
+            jax.ShapeDtypeStruct((8, 128), f32),
         ],
         compiler_params=pltpu.CompilerParams(vmem_limit_bytes=48 * 1024 * 1024),
         name="frames",
-    )(positions, extended, probe, amplitudes, *forward, *inverse)
+    )(positions, extended, probe, amplitudes, *tables)
 
 
 def plan(sizes, rows):
@@ -314,6 +311,7 @@
             stages.append((axis, bit, halved, left, offset))
             offset += left
         plans.append(stages)
+    plans = plans * 2
     return plans, max(stages[-1][3] + stages[-1][4] for stages in plans)
 
 
@@ -384,8 +382,12 @@
                 inner_ref[c, rows, :] = part + jnp.concatenate(pieces, axis=1)
 
     count = len(plans[0])
-    starts = [[0], [0]]
-    flights = [None, None]
+    parts = len(plans)
+    planes = in_ref.shape[1]
+    cut = (planes + 1) // 2
+    bands = [pl.ds(0, cut), pl.ds(0, cut), pl.ds(cut, planes - cut), pl.ds(cut, planes - cut)]
+    starts = [[0] for _ in plans]
+    flights = [None] * parts
 
     def send(part, stage):
         axis, bit, halved, size, offset = plans[part][stage]
@@ -396,8 +398,8 @@
         kept = pl.multiple_of(start + mine * size, 8) if halved else start
         starts[part].append(kept)
         copy = pltpu.make_async_remote_copy(
-            src_ref=source.at[part, :, pl.ds(gone, size), :],
-            dst_ref=landed.at[part, :, pl.ds(offset, size), :],
+            src_ref=source.at[part % 2, bands[part], pl.ds(gone, size), :],
+            dst_ref=landed.at[part % 2, bands[part], pl.ds(offset, size), :],
             send_sem=send_rs.at[part, stage],
             recv_sem=recv_rs.at[part, stage],
             device_id=partner(axis, bit),
@@ -412,8 +414,9 @@
         source = in_ref if stage == 0 else partial
         rows = pl.ds(starts[part][-1], size)
         target = out_ref if stage == count - 1 else partial
-        target[part, :, rows, :] = (
-            source[part, :, rows, :] + landed[part, :, pl.ds(offset, size), :]
+        half, band = part % 2, bands[part]
+        target[half, band, rows, :] = (
+            source[half, band, rows, :] + landed[half, band, pl.ds(offset, size), :]
         )
 
     def spread(part, stage):
@@ -423,8 +426,8 @@
             return
         rows = pl.ds(starts[part][stage + 1], size)
         copy = pltpu.make_async_remote_copy(
-            src_ref=out_ref.at[part, :, rows, :],
-            dst_ref=out_ref.at[part, :, rows, :],
+            src_ref=out_ref.at[part % 2, bands[part], rows, :],
+            dst_ref=out_ref.at[part % 2, bands[part], rows, :],
             send_sem=send_ag.at[part, stage],
             recv_sem=recv_ag.at[part, stage],
             device_id=partner(axis, bit),
@@ -433,20 +436,20 @@
         copy.start()
         flights[part] = copy
 
-    for part in range(2):
+    for part in range(parts):
         send(part, 0)
     swap_starts("row", coords, row_copies)
     for stage in range(count):
         if stage == 1:
             rows_done()
-        for part in range(2):
+        for part in range(parts):
             take(part, stage)
             if stage + 1 < count:
                 send(part, stage + 1)
             else:
                 spread(part, stage)
     for stage in range(count - 2, -2, -1):
-        for part in range(2):
+        for part in range(parts):
             if flights[part] is not None:
                 flights[part].wait()
             if stage >= 0:
@@ -462,7 +465,7 @@
     wide = canvas.shape[2]
     side = wide - 2 * H
     count = len(plans[0])
-    dma = pltpu.SemaphoreType.DMA((parts, count))
+    dma = pltpu.SemaphoreType.DMA((len(plans), count))
     return pl.pallas_call(
         functools.partial(total_kernel, plans),
         out_shape=[
@@ -493,10 +496,9 @@
     object_field = jnp.stack(
         [object_amplitude * jnp.cos(object_phase), object_amplitude * jnp.sin(object_phase)]
     )
-    canvas, sums = frame_terms(positions, extend(object_field), probe, amplitudes)
+    canvas, sums, step_size = frame_terms(positions, extend(object_field), probe, amplitudes)
     total, inner = total_over_mesh(sums, canvas)
-    step_size = 1.0 / (jnp.max(jnp.sum(probe * probe, axis=(0, 1))) + 1e-06)
-    new_object = object_field + inner * step_size
+    new_object = object_field + inner * step_size[0, 0]
     total = jnp.concatenate([total[0], total[1]], axis=-1)
     total_weight = total[-1]
     total_sum = total[:-1].reshape(probe.shape)

time: 121 us -> 109 us (0.901)
  Pallas kernels: 106 us -> 99 us
  other arithmetic: 8.48 us -> 5.35 us
    pallas_call x1, Pallas kernels: 50.8 us -> 46.3 us  [total_over_mesh(): pl.pallas_call(functools.partial(total_kernel, plans), out_shape=[jax.Sha...]
    pallas_call x1, Pallas kernels: 39.6 us -> 36.9 us  [frame_terms(): pl.pallas_call(frames_kernel, grid_spec=pltpu.PrefetchScalarGridSpec(num_...]
    convert_element_type x2 -> x0, other arithmetic: 1.99 us -> none  [the longest x1 1 us: fourier_tables(): imag = (sign * jnp.sin(angle) * norming).astype(jnp.bfloat16)]
    unnamed x5 -> x9, local copies, waits for them, and re-layouts: 3.96 us -> 2.59 us
where the time goes in v4:
time: 109 us; the launch traced here: 108 us
  Pallas kernels  99 us (91%)
  other arithmetic  5.35 us (5%)
  local copies, waits for them, and re-layouts  3.25 us (3%)
    pallas_call x1, Pallas kernels, total_over_mesh(): pl.pallas_call(functools.partial(total_kernel, plans), out_shape=[jax.Sha...  46.3 us
    pallas_call x1, Pallas kernels, frame_terms(): pl.pallas_call(frames_kernel, grid_spec=pltpu.PrefetchScalarGridSpec(num_...  36.9 us
    pallas_call x1, Pallas kernels, extend(): pl.pallas_call(extend_kernel, out_shape=jax.ShapeDtypeStruct((2, wide + 8...  15.8 us
    unnamed x9, local copies, waits for them, and re-layouts  2.59 us

profile of v4, /device:TPU:1, one launch (start us, length us, event | category | flops | bytes accessed | tf_op | source)
XLA Modules:
  0.0 108.4 jit_solution(12895336900717131002)
XLA Ops:
  0.6 0.0 copy-start.2
  0.6 0.0 copy-start.3
  0.7 0.0 copy-start
  0.7 0.9 copy.9.pos_ref
  1.6 2.0 %multiply_bitcast_fusion.1 = (f32[1,256,256]{2,1,0:T(8,128)S(1)}, f32[1,256,256]{2,1,0:T(8,128)S(1)}) fusion(f32[256,256]{1,0:T(8,128)} %param.7, f32[256,256]{1,0:T(8,128)} %param.8), kind=kLoop, calls=%fused_computation.11 | loop fusion | flops 131072 | bytes 1048576 | tf_op jit(solution)/shard_map/stack | solution.py:496
  3.6 15.8 %extend.1.ext_ref = f32[2,392,384]{2,1,0:T(8,128)S(1)} custom-call(f32[2,256,256]{2,1,0:T(8,128)S(1)} %pad_maximum_fusion.tile_ref), custom_call_target="tpu_custom_call" | custom-call | tf_op jit(solution)/shard_map/extend/pallas_call | solution.py:119
  19.4 0.0 copy-done.2
  19.4 0.0 copy-done.3
  19.4 0.0 copy-done
  19.4 36.9 %frames.1 = (f32[2,392,384]{2,1,0:T(8,128)S(1)}, f32[2,9,256,128]{3,2,1,0:T(8,128)}, f32[8,128]{1,0:T(8,128)S(1)}) custom-call(s32[8,2]{1,0:T(8,128)S(1)} %copy.9.pos_ref, f32[2,392,384]{2,1,0:T(8,128)S(1)} %extend.1.ext_ref, f32[4,2,256,256]{3,2,1,0:T(8,128)S(1)} %copy-done, f32[8,256,256]{2,1,0:T(8,128)} %amp_ref.1, bf16[512,512]{1,0:T(8,128)(2,1)S(1)} %copy-done.3, ...), custom_call_target="tpu_custom_call" | custom-call | tf_op jit(solution)/shard_map/frames/pallas_call | solution.py:267
  56.4 0.5 slice.15
  56.9 0.0 copy-start.1
  56.9 1.7 %copy-done.1 = f32[2,9,256,128]{3,2,1,0:T(8,128)S(1)} copy-done((f32[2,9,256,128]{3,2,1,0:T(8,128)S(1)}, f32[2,9,256,128]{3,2,1,0:T(8,128)}, u32[]{:S(2)}) %copy-start.1) | copy-done | bytes 2359320
  58.5 46.3 %total.1 = (f32[2,9,256,128]{3,2,1,0:T(8,128)S(1)}, f32[2,256,256]{2,1,0:T(8,128)S(1)}) custom-call(f32[2,9,256,128]{3,2,1,0:T(8,128)S(1)} %copy-done.1, f32[2,392,384]{2,1,0:T(8,128)S(1)} %get-tuple-element.8.canvas_ref), custom_call_target="tpu_custom_call" | custom-call | tf_op jit(solution)/shard_map/total/pallas_call | solution.py:469
  104.9 1.5 %multiply_add_fusion = f32[2,256,256]{2,1,0:T(8,128)} fusion(f32[2,256,256]{2,1,0:T(8,128)S(1)} %get-tuple-element.9, f32[]{:T(128)} %bitcast.2, f32[1,256,256]{2,1,0:T(8,128)S(1)} %get-tuple-element.17, f32[1,256,256]{2,1,0:T(8,128)S(1)} %get-tuple-element.16), kind=kLoop, calls=%fused_computation.7 | loop fusion | flops 393216 | bytes 1572868 | tf_op jit(solution)/shard_map/add | solution.py:501
  106.4 0.2 slice_bitcast_fusion
  106.6 0.1 fusion
  106.7 1.6 %divide_add_fusion = f32[4,2,256,256]{3,2,1,0:T(8,128)} fusion(f32[4,2,256,256]{3,2,1,0:T(8,128)S(1)} %copy-done, f32[4,2,256,256]{3,2,1,0:T(8,128)S(1)} %bitcast.13, f32[256,256]{1,0:T(8,128)S(1)} %get-tuple-element.12, f32[256,256]{1,0:T(8,128)S(1)} %get-tuple-element.13), kind=kLoop, calls=%fused_computation.3 | loop fusion | flops 2097152 | bytes 6815744 | tf_op jit(solution)/shard_map/add | solution.py:505
  (2 shorter events, 0.1 us)
Async XLA Ops:
  0.6 18.8 %copy-start.2 = (bf16[512,512]{1,0:T(8,128)(2,1)S(1)}, bf16[512,512]{1,0:T(8,128)(2,1)}, u32[]{:S(2)}) copy-start(bf16[512,512]{1,0:T(8,128)(2,1)} %constant.7.clone.right_ref) | copy-start | bytes 1572868
  0.6 18.8 %copy-start.3 = (bf16[512,512]{1,0:T(8,128)(2,1)S(1)}, bf16[512,512]{1,0:T(8,128)(2,1)}, u32[]{:S(2)}) copy-start(bf16[512,512]{1,0:T(8,128)(2,1)} %constant.6.clone.left_ref) | copy-start | bytes 1572868
  0.7 18.7 %copy-start = (f32[4,2,256,256]{3,2,1,0:T(8,128)S(1)}, f32[4,2,256,256]{3,2,1,0:T(8,128)}, u32[]{:S(2)}) copy-start(f32[4,2,256,256]{3,2,1,0:T(8,128)} %probe_ref.1) | copy-start | bytes 6291460
  56.9 1.7 %copy-start.1 = (f32[2,9,256,128]{3,2,1,0:T(8,128)S(1)}, f32[2,9,256,128]{3,2,1,0:T(8,128)}, u32[]{:S(2)}) copy-start(f32[2,9,256,128]{3,2,1,0:T(8,128)} %get-tuple-element.7.in_ref) | copy-start | bytes 7077892

commit v5 on v4

--- a/solution.py
+++ b/solution.py
@@ -311,7 +311,7 @@
             stages.append((axis, bit, halved, left, offset))
             offset += left
         plans.append(stages)
-    plans = plans * 2
+    plans = plans * 3
     return plans, max(stages[-1][3] + stages[-1][4] for stages in plans)
 
 
@@ -384,8 +384,8 @@
     count = len(plans[0])
     parts = len(plans)
     planes = in_ref.shape[1]
-    cut = (planes + 1) // 2
-    bands = [pl.ds(0, cut), pl.ds(0, cut), pl.ds(cut, planes - cut), pl.ds(cut, planes - cut)]
+    cuts = [planes * k // 3 for k in range(4)]
+    bands = [pl.ds(cuts[p // 2], cuts[p // 2 + 1] - cuts[p // 2]) for p in range(parts)]
     starts = [[0] for _ in plans]
     flights = [None] * parts
 

time: 109 us -> 108 us (level)
  Pallas kernels: 99 us -> 97.8 us
    pallas_call x1, Pallas kernels: 46.3 us -> 45.1 us  [total_over_mesh(): pl.pallas_call(functools.partial(total_kernel, plans), out_shape=[jax.Sha...]
where the time goes in v5:
time: 108 us; the launch traced here: 107 us
  Pallas kernels  97.8 us (91%)
  other arithmetic  5.35 us (5%)
  local copies, waits for them, and re-layouts  3.25 us (3%)
    pallas_call x1, Pallas kernels, total_over_mesh(): pl.pallas_call(functools.partial(total_kernel, plans), out_shape=[jax.Sha...  45.1 us
    pallas_call x1, Pallas kernels, frame_terms(): pl.pallas_call(frames_kernel, grid_spec=pltpu.PrefetchScalarGridSpec(num_...  36.9 us
    pallas_call x1, Pallas kernels, extend(): pl.pallas_call(extend_kernel, out_shape=jax.ShapeDtypeStruct((2, wide + 8...  15.8 us
    unnamed x9, local copies, waits for them, and re-layouts  2.59 us

profile of v5, /device:TPU:1, one launch (start us, length us, event | category | flops | bytes accessed | tf_op | source)
XLA Modules:
  0.0 107.2 jit_solution(17320416957029191315)
XLA Ops:
  0.6 0.0 copy-start.2
  0.6 0.0 copy-start.3
  0.7 0.0 copy-start
  0.7 0.9 copy.9.pos_ref
  1.6 2.0 %multiply_bitcast_fusion.1 = (f32[1,256,256]{2,1,0:T(8,128)S(1)}, f32[1,256,256]{2,1,0:T(8,128)S(1)}) fusion(f32[256,256]{1,0:T(8,128)} %param.7, f32[256,256]{1,0:T(8,128)} %param.8), kind=kLoop, calls=%fused_computation.11 | loop fusion | flops 131072 | bytes 1048576 | tf_op jit(solution)/shard_map/stack | solution.py:496
  3.6 15.8 %extend.1.ext_ref = f32[2,392,384]{2,1,0:T(8,128)S(1)} custom-call(f32[2,256,256]{2,1,0:T(8,128)S(1)} %pad_maximum_fusion.tile_ref), custom_call_target="tpu_custom_call" | custom-call | tf_op jit(solution)/shard_map/extend/pallas_call | solution.py:119
  19.4 0.0 copy-done.2
  19.4 0.0 copy-done.3
  19.4 0.0 copy-done
  19.4 36.9 %frames.1 = (f32[2,392,384]{2,1,0:T(8,128)S(1)}, f32[2,9,256,128]{3,2,1,0:T(8,128)}, f32[8,128]{1,0:T(8,128)S(1)}) custom-call(s32[8,2]{1,0:T(8,128)S(1)} %copy.9.pos_ref, f32[2,392,384]{2,1,0:T(8,128)S(1)} %extend.1.ext_ref, f32[4,2,256,256]{3,2,1,0:T(8,128)S(1)} %copy-done, f32[8,256,256]{2,1,0:T(8,128)} %amp_ref.1, bf16[512,512]{1,0:T(8,128)(2,1)S(1)} %copy-done.3, ...), custom_call_target="tpu_custom_call" | custom-call | tf_op jit(solution)/shard_map/frames/pallas_call | solution.py:267
  56.4 0.5 slice.15
  56.9 0.0 copy-start.1
  56.9 1.7 %copy-done.1 = f32[2,9,256,128]{3,2,1,0:T(8,128)S(1)} copy-done((f32[2,9,256,128]{3,2,1,0:T(8,128)S(1)}, f32[2,9,256,128]{3,2,1,0:T(8,128)}, u32[]{:S(2)}) %copy-start.1) | copy-done | bytes 2359320
  58.5 45.1 %total.1 = (f32[2,9,256,128]{3,2,1,0:T(8,128)S(1)}, f32[2,256,256]{2,1,0:T(8,128)S(1)}) custom-call(f32[2,9,256,128]{3,2,1,0:T(8,128)S(1)} %copy-done.1, f32[2,392,384]{2,1,0:T(8,128)S(1)} %get-tuple-element.8.canvas_ref), custom_call_target="tpu_custom_call" | custom-call | tf_op jit(solution)/shard_map/total/pallas_call | solution.py:469
  103.6 1.5 %multiply_add_fusion = f32[2,256,256]{2,1,0:T(8,128)} fusion(f32[2,256,256]{2,1,0:T(8,128)S(1)} %get-tuple-element.9, f32[]{:T(128)} %bitcast.2, f32[1,256,256]{2,1,0:T(8,128)S(1)} %get-tuple-element.17, f32[1,256,256]{2,1,0:T(8,128)S(1)} %get-tuple-element.16), kind=kLoop, calls=%fused_computation.7 | loop fusion | flops 393216 | bytes 1572868 | tf_op jit(solution)/shard_map/add | solution.py:501
  105.2 0.2 slice_bitcast_fusion
  105.4 0.1 fusion
  105.5 1.6 %divide_add_fusion = f32[4,2,256,256]{3,2,1,0:T(8,128)} fusion(f32[4,2,256,256]{3,2,1,0:T(8,128)S(1)} %copy-done, f32[4,2,256,256]{3,2,1,0:T(8,128)S(1)} %bitcast.13, f32[256,256]{1,0:T(8,128)S(1)} %get-tuple-element.12, f32[256,256]{1,0:T(8,128)S(1)} %get-tuple-element.13), kind=kLoop, calls=%fused_computation.3 | loop fusion | flops 2097152 | bytes 6815744 | tf_op jit(solution)/shard_map/add | solution.py:505
  (2 shorter events, 0.1 us)
Async XLA Ops:
  0.6 18.8 %copy-start.2 = (bf16[512,512]{1,0:T(8,128)(2,1)S(1)}, bf16[512,512]{1,0:T(8,128)(2,1)}, u32[]{:S(2)}) copy-start(bf16[512,512]{1,0:T(8,128)(2,1)} %constant.7.clone.right_ref) | copy-start | bytes 1572868
  0.6 18.8 %copy-start.3 = (bf16[512,512]{1,0:T(8,128)(2,1)S(1)}, bf16[512,512]{1,0:T(8,128)(2,1)}, u32[]{:S(2)}) copy-start(bf16[512,512]{1,0:T(8,128)(2,1)} %constant.6.clone.left_ref) | copy-start | bytes 1572868
  0.7 18.7 %copy-start = (f32[4,2,256,256]{3,2,1,0:T(8,128)S(1)}, f32[4,2,256,256]{3,2,1,0:T(8,128)}, u32[]{:S(2)}) copy-start(f32[4,2,256,256]{3,2,1,0:T(8,128)} %probe_ref.1) | copy-start | bytes 6291460
  56.9 1.7 %copy-start.1 = (f32[2,9,256,128]{3,2,1,0:T(8,128)S(1)}, f32[2,9,256,128]{3,2,1,0:T(8,128)}, u32[]{:S(2)}) copy-start(f32[2,9,256,128]{3,2,1,0:T(8,128)} %get-tuple-element.7.in_ref) | copy-start | bytes 7077892
